TPU v7x, 128 devices: a whole 4x4x4 slice. The times are simulated.
128 devices in a mesh: dp: 128 (over x, y, z, core).
Axes of the slice: x: 4, y: 4, z: 4, core: 2. Of those that a mesh axis runs over, the one named last changes fastest.
Arguments:
- query_emb: bfloat16 [16384, 1024], P('dp'), may hold values from -0.1875 to 0.1875
- doc_emb: bfloat16 [16384, 1024], P('dp'), may hold values from -0.1875 to 0.1875
- pair_blocks: int32 [128, 4, 2], replicated, may hold values from 0 to 127, as said below
- active_pair_count: int32 [128], replicated, may hold values from 0 to 4, as said below
Outputs:
- grad_query: float32 [16384, 1024], P('dp')
- grad_doc: float32 [16384, 1024], P('dp')
Inputs may be any that keep to these rules, and one draw needn't show every extreme that they name: `pair_blocks`: the live slots of all owners together name every row block exactly 2 times as a row block, never pair a block with itself, and never repeat a tile; slots that are not live hold arbitrary block indices. `active_pair_count`: the counts sum to 256, and some owner has 4.
All inputs are finite; a program needn't handle non-finite values.
Results may differ from a plain program's by a relative error of at most 0.005.
Values may be sent and summed in bfloat16 or wider, within the bound.
No kernel may reach another device: no remote copies, remote signals or barrier semaphores. Data moves between devices by JAX's collectives and lax.ppermute only.
A program may use at most 64 MiB of HBM per device.

v0:
```python
import jax
import jax.numpy as jnp
from jax import lax
from jax.sharding import PartitionSpec as P

LOGIT_SCALE = 64.0
EPSILON = 1e-06


def unit_rows(raw_rows):
    widened = raw_rows.astype(jnp.float32)
    inverse = lax.rsqrt(jnp.sum(widened * widened, axis=1) + EPSILON)
    return (widened, inverse, (widened * inverse[:, None]).astype(jnp.bfloat16))


def unit_grad(widened, inverse, upstream):
    radial = jnp.sum(widened * upstream, axis=1)
    return upstream * inverse[:, None] - widened * (radial * inverse * inverse * inverse)[:, None]


def on_device(query_emb, doc_emb, pair_blocks, active_pair_count):
    devices = lax.axis_size("dp")
    current_owner = lax.axis_index("dp")
    row_count, feature_width = query_emb.shape
    piece_rows = row_count // devices
    query_wide, query_inverse, query_unit = unit_rows(query_emb)
    doc_wide, doc_inverse, doc_unit = unit_rows(doc_emb)
    every_slot = pair_blocks.shape[1]
    active_flags = (jnp.arange(every_slot)[None, :] < active_pair_count[:, None]).astype(
        jnp.float32
    )
    slot_count = pair_blocks.shape[1]
    want_rows = pair_blocks[:, :, 0]
    want_cols = pair_blocks[:, :, 1]
    my_rows = lax.dynamic_index_in_dim(want_rows, current_owner, 0, keepdims=False)
    my_cols = lax.dynamic_index_in_dim(want_cols, current_owner, 0, keepdims=False)
    local_active = lax.dynamic_index_in_dim(active_flags, current_owner, 0, keepdims=False)
    block_ids = jnp.arange(devices)
    spread_query, spread_doc = (
        lax.all_to_all(
            query_unit.reshape(devices, piece_rows, feature_width),
            "dp",
            split_axis=0,
            concat_axis=0,
            tiled=True,
        ),
        lax.all_to_all(
            doc_unit.reshape(devices, piece_rows, feature_width),
            "dp",
            split_axis=0,
            concat_axis=0,
            tiled=True,
        ),
    )
    fetched_query, fetched_doc = (
        lax.all_to_all(spread_query[want_rows], "dp", split_axis=0, concat_axis=2, tiled=True),
        lax.all_to_all(spread_doc[want_cols], "dp", split_axis=0, concat_axis=2, tiled=True),
    )
    fetched_query = fetched_query.reshape(slot_count, row_count, feature_width)
    fetched_doc = fetched_doc.reshape(slot_count, row_count, feature_width)
    tile_scores = LOGIT_SCALE * jnp.einsum(
        "kid,kjd->kij", fetched_query, fetched_doc, preferred_element_type=jnp.float32
    )
    tile_exp = jnp.exp(tile_scores)
    row_part = jnp.sum(tile_exp, axis=2) * local_active[:, None]
    col_part = jnp.sum(tile_exp, axis=1) * local_active[:, None]
    own_scores = LOGIT_SCALE * jnp.einsum(
        "id,jd->ij", query_unit, doc_unit, preferred_element_type=jnp.float32
    )
    own_exp = jnp.exp(own_scores)
    own_row = jnp.sum(own_exp, axis=1)
    own_col = jnp.sum(own_exp, axis=0)
    row_hot = (my_rows[:, None] == block_ids[None, :]).astype(jnp.float32)
    col_hot = (my_cols[:, None] == block_ids[None, :]).astype(jnp.float32)
    self_hot = (block_ids == current_owner).astype(jnp.float32)
    row_table = (
        jnp.einsum("kb,kr->br", row_hot, row_part, precision=lax.Precision.HIGHEST)
        + self_hot[:, None] * own_row[None, :]
    )
    col_table = (
        jnp.einsum("kb,kr->br", col_hot, col_part, precision=lax.Precision.HIGHEST)
        + self_hot[:, None] * own_col[None, :]
    )
    row_total, col_total = lax.psum((row_table, col_table), "dp")
    row_lse_all = jnp.log(row_total)
    col_lse_all = jnp.log(col_total)
    slot_row_lse = row_lse_all[my_rows]
    slot_col_lse = col_lse_all[my_cols]
    own_row_lse = lax.dynamic_index_in_dim(row_lse_all, current_owner, 0, keepdims=False)
    own_col_lse = lax.dynamic_index_in_dim(col_lse_all, current_owner, 0, keepdims=False)
    half_sum = 0.5 * (
        jnp.exp(tile_scores - slot_row_lse[:, :, None])
        + jnp.exp(tile_scores - slot_col_lse[:, None, :])
    )
    tile_weight = half_sum.astype(jnp.bfloat16)
    query_part = (
        LOGIT_SCALE
        * jnp.einsum("kij,kjd->kid", tile_weight, fetched_doc, preferred_element_type=jnp.float32)
    ).astype(jnp.bfloat16)
    doc_part = (
        LOGIT_SCALE
        * jnp.einsum("kij,kid->kjd", tile_weight, fetched_query, preferred_element_type=jnp.float32)
    ).astype(jnp.bfloat16)
    own_half = 0.5 * (
        jnp.exp(own_scores - own_row_lse[:, None]) + jnp.exp(own_scores - own_col_lse[None, :])
    )
    own_weight = (own_half - jnp.eye(row_count, dtype=jnp.float32)).astype(jnp.bfloat16)
    own_query = (
        LOGIT_SCALE
        * jnp.einsum("ij,jd->id", own_weight, doc_unit, preferred_element_type=jnp.float32)
    ).astype(jnp.bfloat16)
    own_doc = (
        LOGIT_SCALE
        * jnp.einsum("ij,id->jd", own_weight, query_unit, preferred_element_type=jnp.float32)
    ).astype(jnp.bfloat16)
    piece_query, piece_doc = (
        lax.all_to_all(
            query_part.reshape(slot_count, devices, piece_rows, feature_width),
            "dp",
            split_axis=1,
            concat_axis=1,
            tiled=True,
        ),
        lax.all_to_all(
            doc_part.reshape(slot_count, devices, piece_rows, feature_width),
            "dp",
            split_axis=1,
            concat_axis=1,
            tiled=True,
        ),
    )
    route_rows = (
        (want_rows.T[:, :, None] == block_ids[None, None, :]).astype(jnp.float32)
        * active_flags.T[:, :, None]
    ).astype(jnp.bfloat16)
    route_cols = (
        (want_cols.T[:, :, None] == block_ids[None, None, :]).astype(jnp.float32)
        * active_flags.T[:, :, None]
    ).astype(jnp.bfloat16)
    sum_query = jnp.einsum(
        "kob,kord->brd", route_rows, piece_query, preferred_element_type=jnp.float32
    )
    sum_doc = jnp.einsum("kob,kord->brd", route_cols, piece_doc, preferred_element_type=jnp.float32)
    home_query, home_doc = (
        lax.all_to_all(
            sum_query.astype(jnp.bfloat16), "dp", split_axis=0, concat_axis=0, tiled=True
        ).astype(sum_query.dtype),
        lax.all_to_all(
            sum_doc.astype(jnp.bfloat16), "dp", split_axis=0, concat_axis=0, tiled=True
        ).astype(sum_doc.dtype),
    )
    query_grad_unit = own_query.astype(jnp.float32) + home_query.reshape(row_count, feature_width)
    doc_grad_unit = own_doc.astype(jnp.float32) + home_doc.reshape(row_count, feature_width)
    grad_query = unit_grad(query_wide, query_inverse, query_grad_unit)
    grad_doc = unit_grad(doc_wide, doc_inverse, doc_grad_unit)
    return (grad_query, grad_doc)


def solution(mesh):
    return jax.shard_map(
        on_device,
        mesh=mesh,
        in_specs=(P("dp", None), P("dp", None), P(), P()),
        out_specs=(P("dp", None), P("dp", None)),
        check_vma=False,
    )
```

profile of v0, /device:TPU:1, one launch (start us, length us, event | category | flops | bytes accessed | tf_op | source)
XLA Modules:
  0.0 335.5 jit_solution(1779194523067814615)
XLA Ops:
  12.5 11.5 %all-to-all-start = ((bf16[128,2,512]{2,1,0:T(2,128)(2,1)}), bf16[128,2,512]{2,1,0:T(2,128)(2,1)S(1)}, u32[]{:S(2)}, u32[]{:S(2)}) async-start(bf16[128,2,512]{2,1,0:T(2,128)(2,1)} %reshape.229), calls=%async_computation | async-start | bytes 524288 | tf_op jit(solution)/shard_map/all_to_all | solution.py:40
  25.7 9.1 %all-to-all-done = bf16[128,2,512]{2,1,0:T(2,128)(2,1)S(1)} async-done(((bf16[128,2,512]{2,1,0:T(2,128)(2,1)}), bf16[128,2,512]{2,1,0:T(2,128)(2,1)S(1)}, u32[]{:S(2)}, u32[]{:S(2)}) %all-to-all-start) | async-done | bytes 262176 | tf_op jit(solution)/shard_map/all_to_all | solution.py:40
  34.8 4.7 %all-to-all-start.2 = ((bf16[128,2,512]{2,1,0:T(2,128)(2,1)}), bf16[128,2,512]{2,1,0:T(2,128)(2,1)S(1)}, u32[]{:S(2)}, u32[]{:S(2)}) async-start(bf16[128,2,512]{2,1,0:T(2,128)(2,1)} %reshape.227), calls=%async_computation.2 | async-start | bytes 524288 | tf_op jit(solution)/shard_map/all_to_all | solution.py:47
  40.1 2.1 gather_fusion
  42.2 1.3 reshape.182
  43.4 6.9 %all-to-all-done.2 = bf16[128,2,512]{2,1,0:T(2,128)(2,1)S(1)} async-done(((bf16[128,2,512]{2,1,0:T(2,128)(2,1)}), bf16[128,2,512]{2,1,0:T(2,128)(2,1)S(1)}, u32[]{:S(2)}, u32[]{:S(2)}) %all-to-all-start.2) | async-done | bytes 262176 | tf_op jit(solution)/shard_map/all_to_all | solution.py:47
  50.4 4.7 %all-to-all-start.1 = ((bf16[128,4,1,1024]{3,1,2,0:T(4,128)(2,1)}), bf16[128,4,1,1024]{3,1,2,0:T(4,128)(2,1)S(1)}, u32[]{:S(2)}, u32[]{:S(2)}) async-start(bf16[128,4,1,1024]{3,1,2,0:T(4,128)(2,1)} %bitcast.1), calls=%async_computation.1 | async-start | bytes 2097152 | tf_op jit(solution)/shard_map/all_to_all | solution.py:56
  55.6 2.1 gather_fusion.1
  57.7 1.2 reshape.192
  58.9 15.4 %all-to-all-done.1 = bf16[128,4,1,1024]{3,1,2,0:T(4,128)(2,1)S(1)} async-done(((bf16[128,4,1,1024]{3,1,2,0:T(4,128)(2,1)}), bf16[128,4,1,1024]{3,1,2,0:T(4,128)(2,1)S(1)}, u32[]{:S(2)}, u32[]{:S(2)}) %all-to-all-start.1) | async-done | bytes 1048608 | tf_op jit(solution)/shard_map/all_to_all | solution.py:56
  74.3 4.8 %all-to-all-start.3 = ((bf16[128,4,1,1024]{3,1,2,0:T(4,128)(2,1)}), bf16[128,4,1,1024]{3,1,2,0:T(4,128)(2,1)S(1)}, u32[]{:S(2)}, u32[]{:S(2)}) async-start(bf16[128,4,1,1024]{3,1,2,0:T(4,128)(2,1)} %bitcast.92), calls=%async_computation.3 | async-start | bytes 2097152 | tf_op jit(solution)/shard_map/all_to_all | solution.py:57
  81.2 17.2 %all-to-all-done.3 = bf16[128,4,1,1024]{3,1,2,0:T(4,128)(2,1)S(1)} async-done(((bf16[128,4,1,1024]{3,1,2,0:T(4,128)(2,1)}), bf16[128,4,1,1024]{3,1,2,0:T(4,128)(2,1)S(1)}, u32[]{:S(2)}, u32[]{:S(2)}) %all-to-all-start.3) | async-done | bytes 1048608 | tf_op jit(solution)/shard_map/all_to_all | solution.py:57
  101.2 138.7 %all-reduce.3.cloned.1.call-done = (f32[128,128]{1,0:T(8,128)}, f32[128,128]{1,0:T(8,128)}) async-done(((f32[128,128]{1,0:T(8,128)}, f32[128,128]{1,0:T(8,128)}), (f32[128,128]{1,0:T(8,128)}, f32[128,128]{1,0:T(8,128)})) %all-reduce.3.cloned.1.call-update) | async-done | bytes 131088 | tf_op jit(solution)/shard_map/psum | solution.py:84
  243.6 1.8 copy.37
  245.4 6.5 %all-to-all-start.4 = ((bf16[4,128,1,1024]{3,0,2,1:T(4,128)(2,1)}), bf16[4,128,1,1024]{3,0,2,1:T(4,128)(2,1)}, u32[]{:S(2)}, u32[]{:S(2)}) async-start(bf16[4,128,1,1024]{3,0,2,1:T(4,128)(2,1)} %copy.37), calls=%async_computation.4 | async-start | bytes 2097152 | tf_op jit(solution)/shard_map/all_to_all | solution.py:117
  252.9 1.8 copy.42
  254.7 16.1 %all-to-all-done.4 = bf16[4,128,1,1024]{3,0,2,1:T(4,128)(2,1)} async-done(((bf16[4,128,1,1024]{3,0,2,1:T(4,128)(2,1)}), bf16[4,128,1,1024]{3,0,2,1:T(4,128)(2,1)}, u32[]{:S(2)}, u32[]{:S(2)}) %all-to-all-start.4) | async-done | bytes 1048608 | tf_op jit(solution)/shard_map/all_to_all | solution.py:117
  270.8 4.8 %all-to-all-start.6 = ((bf16[4,128,1,1024]{3,0,2,1:T(4,128)(2,1)}), bf16[4,128,1,1024]{3,0,2,1:T(4,128)(2,1)S(1)}, u32[]{:S(2)}, u32[]{:S(2)}) async-start(bf16[4,128,1,1024]{3,0,2,1:T(4,128)(2,1)} %copy.42), calls=%async_computation.6 | async-start | bytes 2097152 | tf_op jit(solution)/shard_map/all_to_all | solution.py:124
  275.7 2.0 fusion.11
  279.2 15.8 %all-to-all-done.6 = bf16[4,128,1,1024]{3,0,2,1:T(4,128)(2,1)S(1)} async-done(((bf16[4,128,1,1024]{3,0,2,1:T(4,128)(2,1)}), bf16[4,128,1,1024]{3,0,2,1:T(4,128)(2,1)S(1)}, u32[]{:S(2)}, u32[]{:S(2)}) %all-to-all-start.6) | async-done | bytes 1048608 | tf_op jit(solution)/shard_map/all_to_all | solution.py:124
  294.9 4.6 %all-to-all-start.5 = ((bf16[128,2,512]{2,1,0:T(2,128)(2,1)}), bf16[128,2,512]{2,1,0:T(2,128)(2,1)S(1)}, u32[]{:S(2)}, u32[]{:S(2)}) async-start(bf16[128,2,512]{2,1,0:T(2,128)(2,1)} %reshape.231), calls=%async_computation.5 | async-start | bytes 524288 | tf_op jit(solution)/shard_map/all_to_all | solution.py:145
  301.9 8.6 %all-to-all-done.5 = bf16[128,2,512]{2,1,0:T(2,128)(2,1)S(1)} async-done(((bf16[128,2,512]{2,1,0:T(2,128)(2,1)}), bf16[128,2,512]{2,1,0:T(2,128)(2,1)S(1)}, u32[]{:S(2)}, u32[]{:S(2)}) %all-to-all-start.5) | async-done | bytes 262176 | tf_op jit(solution)/shard_map/all_to_all | solution.py:145
  310.5 4.7 %all-to-all-start.7 = ((bf16[128,2,512]{2,1,0:T(2,128)(2,1)}), bf16[128,2,512]{2,1,0:T(2,128)(2,1)S(1)}, u32[]{:S(2)}, u32[]{:S(2)}) async-start(bf16[128,2,512]{2,1,0:T(2,128)(2,1)} %reshape.233), calls=%async_computation.7 | async-start | bytes 524288 | tf_op jit(solution)/shard_map/all_to_all | solution.py:148
  316.0 10.1 %all-to-all-done.7 = bf16[128,2,512]{2,1,0:T(2,128)(2,1)S(1)} async-done(((bf16[128,2,512]{2,1,0:T(2,128)(2,1)}), bf16[128,2,512]{2,1,0:T(2,128)(2,1)S(1)}, u32[]{:S(2)}, u32[]{:S(2)}) %all-to-all-start.7) | async-done | bytes 262176 | tf_op jit(solution)/shard_map/all_to_all | solution.py:148
  (65 shorter events, 24.7 us)
Async XLA Ops:
  9.3 14.7 %copy-start.1 = (bf16[128,1024]{1,0:T(8,128)(2,1)S(1)}, bf16[128,1024]{1,0:T(8,128)(2,1)}, u32[]{:S(2)}) copy-start(bf16[128,1024]{1,0:T(8,128)(2,1)} %param.5) | copy-start | bytes 786436
  12.5 22.3 %all-to-all-start = ((bf16[128,2,512]{2,1,0:T(2,128)(2,1)}), bf16[128,2,512]{2,1,0:T(2,128)(2,1)S(1)}, u32[]{:S(2)}, u32[]{:S(2)}) async-start(bf16[128,2,512]{2,1,0:T(2,128)(2,1)} %reshape.229), calls=%async_computation | async-start | bytes 524288 | tf_op jit(solution)/shard_map/all_to_all | solution.py:40
  24.0 15.5 %copy-start.2 = (s32[128,4,2]{0,2,1:T(2,128)S(1)}, s32[128,4,2]{0,2,1:T(2,128)}, u32[]{:S(2)}) copy-start(s32[128,4,2]{0,2,1:T(2,128)} %param.6) | copy-start | bytes 12292
  34.8 15.5 %all-to-all-start.2 = ((bf16[128,2,512]{2,1,0:T(2,128)(2,1)}), bf16[128,2,512]{2,1,0:T(2,128)(2,1)S(1)}, u32[]{:S(2)}, u32[]{:S(2)}) async-start(bf16[128,2,512]{2,1,0:T(2,128)(2,1)} %reshape.227), calls=%async_computation.2 | async-start | bytes 524288 | tf_op jit(solution)/shard_map/all_to_all | solution.py:47
  50.4 23.9 %all-to-all-start.1 = ((bf16[128,4,1,1024]{3,1,2,0:T(4,128)(2,1)}), bf16[128,4,1,1024]{3,1,2,0:T(4,128)(2,1)S(1)}, u32[]{:S(2)}, u32[]{:S(2)}) async-start(bf16[128,4,1,1024]{3,1,2,0:T(4,128)(2,1)} %bitcast.1), calls=%async_computation.1 | async-start | bytes 2097152 | tf_op jit(solution)/shard_map/all_to_all | solution.py:56
  74.3 4.9 %copy-start.3 = (s32[128]{0:T(128)S(1)}, s32[128]{0:T(128)}, u32[]{:S(2)}) copy-start(s32[128]{0:T(128)} %param.7) | copy-start | bytes 1540
  74.3 6.5 %copy-start = (bf16[128,1024]{1,0:T(8,128)(2,1)S(1)}, bf16[128,1024]{1,0:T(8,128)(2,1)}, u32[]{:S(2)}) copy-start(bf16[128,1024]{1,0:T(8,128)(2,1)} %param.4) | copy-start | bytes 786436
  74.3 24.1 %all-to-all-start.3 = ((bf16[128,4,1,1024]{3,1,2,0:T(4,128)(2,1)}), bf16[128,4,1,1024]{3,1,2,0:T(4,128)(2,1)S(1)}, u32[]{:S(2)}, u32[]{:S(2)}) async-start(bf16[128,4,1,1024]{3,1,2,0:T(4,128)(2,1)} %bitcast.92), calls=%async_computation.3 | async-start | bytes 2097152 | tf_op jit(solution)/shard_map/all_to_all | solution.py:57
  79.1 160.8 %all-reduce.3.cloned.1.call-start = ((), (), s32[]{:S(2)}) async-start(), calls=%async_computation.8 | async-start | bytes 262144 | tf_op jit(solution)/shard_map/psum | solution.py:84
  245.4 25.3 %all-to-all-start.4 = ((bf16[4,128,1,1024]{3,0,2,1:T(4,128)(2,1)}), bf16[4,128,1,1024]{3,0,2,1:T(4,128)(2,1)}, u32[]{:S(2)}, u32[]{:S(2)}) async-start(bf16[4,128,1,1024]{3,0,2,1:T(4,128)(2,1)} %copy.37), calls=%async_computation.4 | async-start | bytes 2097152 | tf_op jit(solution)/shard_map/all_to_all | solution.py:117
  270.8 24.2 %all-to-all-start.6 = ((bf16[4,128,1,1024]{3,0,2,1:T(4,128)(2,1)}), bf16[4,128,1,1024]{3,0,2,1:T(4,128)(2,1)S(1)}, u32[]{:S(2)}, u32[]{:S(2)}) async-start(bf16[4,128,1,1024]{3,0,2,1:T(4,128)(2,1)} %copy.42), calls=%async_computation.6 | async-start | bytes 2097152 | tf_op jit(solution)/shard_map/all_to_all | solution.py:124
  294.9 15.6 %all-to-all-start.5 = ((bf16[128,2,512]{2,1,0:T(2,128)(2,1)}), bf16[128,2,512]{2,1,0:T(2,128)(2,1)S(1)}, u32[]{:S(2)}, u32[]{:S(2)}) async-start(bf16[128,2,512]{2,1,0:T(2,128)(2,1)} %reshape.231), calls=%async_computation.5 | async-start | bytes 524288 | tf_op jit(solution)/shard_map/all_to_all | solution.py:145
  310.5 15.5 %all-to-all-start.7 = ((bf16[128,2,512]{2,1,0:T(2,128)(2,1)}), bf16[128,2,512]{2,1,0:T(2,128)(2,1)S(1)}, u32[]{:S(2)}, u32[]{:S(2)}) async-start(bf16[128,2,512]{2,1,0:T(2,128)(2,1)} %reshape.233), calls=%async_computation.7 | async-start | bytes 524288 | tf_op jit(solution)/shard_map/all_to_all | solution.py:148
Sparse Core Ops, SparseCore 0:
  101.3 138.5 all-reduce.2
where the time goes:
time: 336 us
  waiting for transfers between devices  238 us (71%)
  starting transfers between devices  46.4 us (14%)
  local copies, waits for them, and re-layouts  19.6 us (6%)
  between operations  14.4 us (4%)
  other arithmetic  8.72 us (3%)
  matrix products  8.56 us (3%)
    psum x1, waiting for transfers between devices, on_device(): row_total, col_total = lax.psum((row_table, col_table), 'dp')  139 us
    all_to_all x1, waiting for transfers between devices, on_device(): lax.all_to_all(spread_doc[want_cols], 'dp', split_axis=0, concat_axis=2,...  17.2 us
    all_to_all x1, waiting for transfers between devices, on_device(): lax.all_to_all(query_part.reshape(slot_count, devices, piece_rows, featur...  16.1 us
    all_to_all x1, waiting for transfers between devices, on_device(): lax.all_to_all(doc_part.reshape(slot_count, devices, piece_rows, feature_...  15.8 us
    all_to_all x1, waiting for transfers between devices, on_device(): lax.all_to_all(spread_query[want_rows], 'dp', split_axis=0, concat_axis=2...  15.4 us
    all_to_all x1, starting transfers between devices, on_device(): lax.all_to_all(query_unit.reshape(devices, piece_rows, feature_width), 'd...  11.5 us
    all_to_all x1, waiting for transfers between devices, on_device(): lax.all_to_all(sum_doc.astype(jnp.bfloat16), 'dp', split_axis=0, concat_a...  10.1 us
    all_to_all x1, waiting for transfers between devices, on_device(): lax.all_to_all(query_unit.reshape(devices, piece_rows, feature_width), 'd...  9.1 us
  transfers between devices with their start and end apart: 9, of which 9 were waited for; matrix products, arithmetic and copies ran while one was open for 6% of the time, Pallas kernels for 0%

commit v1 on v0

v1 whole, which is shorter than its diff:
```python
import jax
import jax.numpy as jnp
from jax import lax
from jax.experimental import pallas as pl
from jax.experimental.pallas import tpu as pltpu
from jax.sharding import PartitionSpec as P

LOGIT_SCALE = 64.0
EPSILON = 1e-06
LANES = 128
SUB = 8


def whole(space):
    return pl.BlockSpec(memory_space=space)


def vmem_call(body, outs, n_smem, n_vmem, scratch=(), name=None):
    return pl.pallas_call(
        body,
        out_shape=outs,
        in_specs=[whole(pltpu.SMEM)] * n_smem + [whole(pltpu.VMEM)] * n_vmem,
        out_specs=jax.tree.map(lambda _: whole(pltpu.VMEM), outs),
        scratch_shapes=list(scratch),
        name=name,
    )


def inverse_norm(wide):
    return lax.rsqrt(jnp.sum(wide * wide, axis=1, keepdims=True) + EPSILON)


def from_pieces(pieces, slot):
    row_tiles, col_tiles = pieces.shape[:2]
    return jnp.concatenate(
        [pieces[:, ct, slot].reshape(row_tiles * SUB, LANES) for ct in range(col_tiles)], axis=1
    )


def dot_nt(a, b):
    return lax.dot_general(a, b, (((1,), (1,)), ((), ())), preferred_element_type=jnp.float32)


def dot_tn(a, b):
    return lax.dot_general(a, b, (((0,), (0,)), ((), ())), preferred_element_type=jnp.float32)


def dot_nn(a, b):
    return lax.dot_general(a, b, (((1,), (0,)), ((), ())), preferred_element_type=jnp.float32)


def own_kernel(q_ref, d_ref, qu_ref, du_ref, inv_ref, et_ref):
    q_wide = q_ref[...].astype(jnp.float32)
    d_wide = d_ref[...].astype(jnp.float32)
    q_inv = inverse_norm(q_wide)
    d_inv = inverse_norm(d_wide)
    q = (q_wide * q_inv).astype(jnp.bfloat16)
    d = (d_wide * d_inv).astype(jnp.bfloat16)
    qu_ref[...] = q
    du_ref[...] = d
    lane = lax.broadcasted_iota(jnp.int32, inv_ref.shape, 1)
    inv_ref[...] = jnp.where(lane == 0, q_inv, d_inv)
    et_ref[...] = jnp.exp(LOGIT_SCALE * dot_nt(d, q))


def gather_kernel(cols_ref, spread_ref, out_ref):
    def step(dest, carry):
        first = spread_ref[cols_ref[2 * dest]]
        second = spread_ref[cols_ref[2 * dest + 1]]
        out_ref[dest, 0:SUB, :] = first
        out_ref[dest, SUB : 2 * SUB, :] = second
        return carry

    lax.fori_loop(0, out_ref.shape[0], step, 0, unroll=8)


def split_pair(value, odd):
    high = value.astype(jnp.bfloat16).astype(jnp.float32)
    return jnp.where(odd, value - high, high)


def tiles_kernel(qu_ref, et_own_ref, fetched_ref, send_ref, et_ref, row_ref, dk_ref):
    row_tiles, col_tiles = send_ref.shape[:2]
    q = qu_ref[...]
    pieces = fetched_ref[...].astype(jnp.float32)
    pieces = pieces.reshape(row_tiles, col_tiles, 2, SUB, LANES)
    et_own = et_own_ref[...]
    row_total = jnp.sum(et_own, axis=0, keepdims=True)
    col_own = jnp.sum(et_own, axis=1, keepdims=True)
    ets, cols = [], []
    for k in range(2):
        wide = from_pieces(pieces, k)
        unit = (wide * inverse_norm(wide)).astype(jnp.bfloat16)
        dk_ref[k] = unit
        et = jnp.exp(LOGIT_SCALE * dot_nt(unit, q))
        et_ref[k] = et
        row_total = row_total + jnp.sum(et, axis=0, keepdims=True)
        cols.append(jnp.sum(et, axis=1, keepdims=True))
        ets.append(et)
    row_ref[...] = row_total
    row_inv = 1.0 / row_total
    half = 0.5 * LOGIT_SCALE
    parts = []
    for make in (lambda e: e * row_inv, lambda e: e):
        parts.append([half * dot_nn(make(e).astype(jnp.bfloat16), q) for e in ets])
    for ct in range(col_tiles):
        lanes = slice(ct * LANES, (ct + 1) * LANES)
        for kind in range(2):
            pair = [x[:, lanes].reshape(row_tiles, 1, SUB, LANES) for x in parts[kind]]
            both = jnp.concatenate(pair, axis=1).reshape(row_tiles, 2 * SUB, LANES)
            send_ref[:, ct, 2 * SUB * kind : 2 * SUB * (kind + 1), :] = both.astype(jnp.bfloat16)
    rows = row_tiles * SUB
    lane = lax.broadcasted_iota(jnp.int32, (rows, LANES), 1)
    value = jnp.where(lane < 2, col_own, jnp.where(lane < 4, cols[0], cols[1]))
    scalars = split_pair(value, lane % 2 == 1).reshape(row_tiles, SUB, LANES).astype(jnp.bfloat16)
    for ct in range(col_tiles):
        send_ref[:, ct, 4 * SUB :, :] = scalars


def combine_kernel(cols_ref, recv_ref, out_ref, acc_a, acc_b, acc_t):
    blocks = recv_ref.shape[0]
    acc_a[...] = jnp.zeros_like(acc_a)
    acc_b[...] = jnp.zeros_like(acc_b)
    lane3 = lax.broadcasted_iota(jnp.int32, acc_t.shape, 2)
    own = recv_ref[:, 4 * SUB :, :].astype(jnp.float32)
    acc_t[...] = jnp.where(lane3 < 2, own, 0.0)
    lane = lax.broadcasted_iota(jnp.int32, (SUB, LANES), 1)
    masks = [(lane >= 2) & (lane < 4), (lane >= 4) & (lane < 6)]

    def add(source, carry):
        a = recv_ref[source, 0 : 2 * SUB, :].astype(jnp.float32)
        b = recv_ref[source, 2 * SUB : 4 * SUB, :].astype(jnp.float32)
        t = recv_ref[source, 4 * SUB :, :].astype(jnp.float32)
        for k in range(2):
            col = cols_ref[2 * source + k]
            acc_a[col] = acc_a[col] + a[k * SUB : (k + 1) * SUB]
            acc_b[col] = acc_b[col] + b[k * SUB : (k + 1) * SUB]
            acc_t[col] = acc_t[col] + jnp.where(masks[k], t, 0.0)
        return carry

    lax.fori_loop(0, blocks, add, 0, unroll=8)
    total = jnp.broadcast_to(jnp.sum(acc_t[...], axis=2, keepdims=True), acc_t.shape)
    acc_t[...] = total
    acc_a[...] = acc_a[...] + acc_b[...] / total
    odd = lane % 2 == 1

    def emit(dest, carry):
        value = jnp.where(
            lane < 2,
            acc_t[dest],
            jnp.where(lane < 4, acc_t[cols_ref[2 * dest]], acc_t[cols_ref[2 * dest + 1]]),
        )
        both = jnp.concatenate([acc_a[dest], split_pair(value, odd)], axis=0)
        out_ref[dest] = both.astype(jnp.bfloat16)
        return carry

    lax.fori_loop(0, blocks, emit, 0, unroll=8)


def unit_grad(wide, inverse, upstream):
    radial = jnp.sum(wide * upstream, axis=1, keepdims=True)
    return upstream * inverse - wide * (radial * inverse * inverse * inverse)


def final_kernel(
    q_ref, d_ref, qu_ref, du_ref, inv_ref, et_own_ref, et_ref, row_ref, dk_ref, home_ref, gq_ref, gd_ref
):
    rows, features = q_ref.shape
    row_tiles, col_tiles = rows // SUB, features // LANES
    pieces = home_ref[...].astype(jnp.float32).reshape(row_tiles, col_tiles, 2, SUB, LANES)
    scalars = pieces[:, 0, 1].reshape(rows, LANES)
    totals = [scalars[:, 2 * i : 2 * i + 1] + scalars[:, 2 * i + 1 : 2 * i + 2] for i in range(3)]
    row_inv = 1.0 / row_ref[...]

    def weight(et, total):
        return 0.5 * (et * row_inv + et * (1.0 / total))

    own = weight(et_own_ref[...], totals[0])
    diagonal = lax.broadcasted_iota(jnp.int32, own.shape, 0) == lax.broadcasted_iota(
        jnp.int32, own.shape, 1
    )
    own = (own - jnp.where(diagonal, 1.0, 0.0)).astype(jnp.bfloat16)

    def part(x):
        return (LOGIT_SCALE * x).astype(jnp.bfloat16).astype(jnp.float32)

    query = part(dot_tn(own, du_ref[...]))
    for k in range(2):
        w = weight(et_ref[k], totals[k + 1]).astype(jnp.bfloat16)
        query = query + part(dot_tn(w, dk_ref[k]))
    gq_ref[...] = unit_grad(q_ref[...].astype(jnp.float32), inv_ref[:, 0:1], query)
    doc = part(dot_nn(own, qu_ref[...])) + from_pieces(pieces, 0)
    gd_ref[...] = unit_grad(d_ref[...].astype(jnp.float32), inv_ref[:, 1:2], doc)


def exchange(x):
    return lax.all_to_all(x, "dp", split_axis=0, concat_axis=0, tiled=True)


def row_columns(pair_blocks, active_pair_count, blocks):
    slots = pair_blocks.shape[1]
    live = jnp.arange(slots)[None, :] < active_pair_count[:, None]
    rows = jnp.where(live, pair_blocks[:, :, 0], -1).reshape(1, -1)
    cols = pair_blocks[:, :, 1].reshape(1, -1)
    match = rows == jnp.arange(blocks)[:, None]
    low = jnp.min(jnp.where(match, cols, blocks - 1), axis=1)
    high = jnp.max(jnp.where(match, cols, 0), axis=1)
    return jnp.stack([low, high], axis=1).reshape(-1).astype(jnp.int32)


def on_device(query_emb, doc_emb, pair_blocks, active_pair_count):
    blocks = lax.axis_size("dp")
    rows, features = query_emb.shape
    row_tiles, col_tiles = rows // SUB, features // LANES
    assert row_tiles * col_tiles == blocks
    sds = jax.ShapeDtypeStruct
    bf16, f32 = jnp.bfloat16, jnp.float32

    doc_pieces = doc_emb.reshape(row_tiles, SUB, col_tiles, LANES).transpose(0, 2, 1, 3)
    spread = exchange(doc_pieces.reshape(blocks, SUB, LANES))
    cols = row_columns(pair_blocks, active_pair_count, blocks)
    qu, du, inv, et_own = vmem_call(
        own_kernel,
        (sds((rows, features), bf16), sds((rows, features), bf16), sds((rows, 2), f32), sds((rows, rows), f32)),
        0,
        2,
        name="own",
    )(query_emb, doc_emb)
    wanted = vmem_call(gather_kernel, sds((blocks, 2 * SUB, LANES), bf16), 1, 1, name="gather")(
        cols, spread
    )
    fetched = exchange(wanted)
    send, et, row_total, dk = vmem_call(
        tiles_kernel,
        (
            sds((row_tiles, col_tiles, 5 * SUB, LANES), bf16),
            sds((2, rows, rows), f32),
            sds((1, rows), f32),
            sds((2, rows, features), bf16),
        ),
        0,
        3,
        name="tiles",
    )(qu, et_own, fetched)
    parts = exchange(send.reshape(blocks, 5 * SUB, LANES))
    acc = pltpu.VMEM((blocks, SUB, LANES), f32)
    combined = vmem_call(
        combine_kernel, sds((blocks, 2 * SUB, LANES), bf16), 1, 1, (acc, acc, acc), name="combine"
    )(cols, parts)
    home = exchange(combined)
    return vmem_call(
        final_kernel, (sds((rows, features), f32), sds((rows, features), f32)), 0, 10, name="final"
    )(query_emb, doc_emb, qu, du, inv, et_own, et, row_total, dk, home)


def solution(mesh):
    return jax.shard_map(
        on_device,
        mesh=mesh,
        in_specs=(P("dp", None), P("dp", None), P(), P()),
        out_specs=(P("dp", None), P("dp", None)),
        check_vma=False,
    )
```

time: 336 us -> 103 us (0.31)
  waiting for transfers between devices: 238 us -> 19.3 us
  blocking collectives: 0 us -> 47 us
  starting transfers between devices: 46.4 us -> 16.2 us
  local copies, waits for them, and re-layouts: 19.6 us -> 3.65 us
  Pallas kernels: 0 us -> 14.9 us
  between operations: 14.4 us -> 0.68 us
  matrix products: 8.56 us -> 0 us
  other arithmetic: 8.72 us -> 0.89 us
    psum x1 -> x0, waiting for transfers between devices: 139 us -> none  [on_device(): row_total, col_total = lax.psum((row_table, col_table), 'dp')]
    all_to_all x8 -> x2, waiting for transfers between devices: 99.1 us -> 19.3 us  [exchange(): return lax.all_to_all(x, 'dp', split_axis=0, concat_axis=0, tiled=True)]
    all_to_all x0 -> x2, blocking collectives: none -> 47 us  [exchange(): return lax.all_to_all(x, 'dp', split_axis=0, concat_axis=0, tiled=True)]
    all_to_all x8 -> x2, starting transfers between devices: 46.4 us -> 16.2 us  [exchange(): return lax.all_to_all(x, 'dp', split_axis=0, concat_axis=0, tiled=True)]
    pallas_call x0 -> x5, Pallas kernels: none -> 14.9 us  [the longest x1 4.08 us: on_device(): vmem_call(combine_kernel, sds((blocks, 2 * SUB, LANES), bf16), 1, 1, (acc...]
    dot_general x10 -> x0, matrix products: 8.56 us -> none  [the longest x1 1.97 us: on_device(): jnp.einsum('kob,kord->brd', route_rows, piece_query, preferred_element_ty...]
    gather x6 -> x0, local copies, waits for them, and re-layouts: 7.72 us -> none  [the longest x2 3.31 us: on_device(): spread_query[want_rows]]
    reshape x3 -> x1, local copies, waits for them, and re-layouts: 4.12 us -> 0.72 us  [row_columns(): return jnp.stack([low, high], axis=1).reshape(-1).astype(jnp.int32)]
  transfers between devices with their start and end apart: 9 -> 2, of which waited for: 9 -> 2; matrix products, arithmetic and copies ran while one was open for 6% -> 3% of each run, Pallas kernels for 0% -> 2%
where the time goes in v1:
time: 103 us
  blocking collectives  47 us (46%)
  waiting for transfers between devices  19.3 us (19%)
  starting transfers between devices  16.2 us (16%)
  Pallas kernels  14.9 us (14%)
  local copies, waits for them, and re-layouts  3.65 us (4%)
    all_to_all x2, blocking collectives, exchange(): return lax.all_to_all(x, 'dp', split_axis=0, concat_axis=0, tiled=True)  47 us
    all_to_all x2, waiting for transfers between devices, exchange(): return lax.all_to_all(x, 'dp', split_axis=0, concat_axis=0, tiled=True)  19.3 us
    all_to_all x2, starting transfers between devices, exchange(): return lax.all_to_all(x, 'dp', split_axis=0, concat_axis=0, tiled=True)  16.2 us
    pallas_call x1, Pallas kernels, on_device(): vmem_call(combine_kernel, sds((blocks, 2 * SUB, LANES), bf16), 1, 1, (acc...  4.08 us
    pallas_call x1, Pallas kernels, on_device(): vmem_call(final_kernel, (sds((rows, features), f32), sds((rows, features)...  3.54 us
    pallas_call x1, Pallas kernels, on_device(): vmem_call(tiles_kernel, (sds((row_tiles, col_tiles, 5 * SUB, LANES), bf16...  3.11 us
    pallas_call x1, Pallas kernels, on_device(): vmem_call(gather_kernel, sds((blocks, 2 * SUB, LANES), bf16), 1, 1, name=...  2.1 us
  transfers between devices with their start and end apart: 2, of which 2 were waited for; matrix products, arithmetic and copies ran while one was open for 3% of the time, Pallas kernels for 2%

profile of v1, /device:TPU:1, one launch (start us, length us, event | category | flops | bytes accessed | tf_op | source)
XLA Modules:
  0.0 102.5 jit_solution(3274286106352277816)
XLA Ops:
  0.6 11.5 %all-to-all-start = ((bf16[128,8,128]{2,1,0:T(8,128)(2,1)}), bf16[128,8,128]{2,1,0:T(8,128)(2,1)S(1)}, u32[]{:S(2)}, u32[]{:S(2)}) async-start(bf16[128,8,128]{2,1,0:T(8,128)(2,1)} %bitcast.12), calls=%async_computation | async-start | bytes 524288 | tf_op jit(solution)/shard_map/all_to_all | solution.py:197
  12.1 0.8 fusion
  12.9 0.7 iota_compare_fusion.1
  13.6 0.1 lt.23
  13.8 0.1 copy.9
  13.9 0.1 squeeze.3
  14.0 0.1 copy.10
  14.1 0.1 broadcast_in_dim.28
  14.2 0.1 select_reduce_fusion.1
  14.4 0.1 copy.11
  14.5 0.7 reshape.38.cols_ref
  15.2 7.7 %all-to-all-done.spread_ref = bf16[128,8,128]{2,1,0:T(8,128)(2,1)S(1)} async-done(((bf16[128,8,128]{2,1,0:T(8,128)(2,1)}), bf16[128,8,128]{2,1,0:T(8,128)(2,1)S(1)}, u32[]{:S(2)}, u32[]{:S(2)}) %all-to-all-start) | async-done | bytes 262176 | tf_op jit(solution)/shard_map/all_to_all | solution.py:197
  22.9 0.0 copy-start.1
  22.9 0.7 copy-done.1
  23.6 2.1 %gather.1 = bf16[128,16,128]{2,1,0:T(8,128)(2,1)} custom-call(s32[256]{0:T(256)} %reshape.38.cols_ref, bf16[128,8,128]{2,1,0:T(8,128)(2,1)} %copy-done.1), custom_call_target="tpu_custom_call" | custom-call | tf_op jit(solution)/shard_map/gather/pallas_call | solution.py:229
  25.7 4.7 %all-to-all-start.1 = ((bf16[128,16,128]{2,1,0:T(8,128)(2,1)}), bf16[128,16,128]{2,1,0:T(8,128)(2,1)S(1)}, u32[]{:S(2)}, u32[]{:S(2)}) async-start(bf16[128,16,128]{2,1,0:T(8,128)(2,1)} %gather.1), calls=%async_computation.1 | async-start | bytes 1048576 | tf_op jit(solution)/shard_map/all_to_all | solution.py:197
  30.5 2.0 %own.1 = (bf16[128,1024]{1,0:T(8,128)(2,1)}, bf16[128,1024]{1,0:T(8,128)(2,1)}, f32[128,2]{1,0:T(8,128)}, f32[128,128]{1,0:T(8,128)}) custom-call(bf16[128,1024]{1,0:T(8,128)(2,1)} %q_ref.3, bf16[128,1024]{1,0:T(8,128)(2,1)} %d_ref.3), custom_call_target="tpu_custom_call" | custom-call | tf_op jit(solution)/shard_map/own/pallas_call | solution.py:222
  32.5 11.6 %all-to-all-done.1.fetched_ref = bf16[128,16,128]{2,1,0:T(8,128)(2,1)S(1)} async-done(((bf16[128,16,128]{2,1,0:T(8,128)(2,1)}), bf16[128,16,128]{2,1,0:T(8,128)(2,1)S(1)}, u32[]{:S(2)}, u32[]{:S(2)}) %all-to-all-start.1) | async-done | bytes 524320 | tf_op jit(solution)/shard_map/all_to_all | solution.py:197
  44.0 0.8 copy-done
  44.8 3.1 %tiles.1 = (bf16[16,8,40,128]{3,2,1,0:T(8,128)(2,1)}, f32[2,128,128]{2,1,0:T(8,128)}, f32[1,128]{1,0:T(1,128)}, bf16[2,128,1024]{2,1,0:T(8,128)(2,1)}) custom-call(bf16[128,1024]{1,0:T(8,128)(2,1)} %get-tuple-element.10.qu_ref, f32[128,128]{1,0:T(8,128)} %get-tuple-element.13.et_own_ref, bf16[128,16,128]{2,1,0:T(8,128)(2,1)} %copy-done), custom_call_target="tpu_custom_call" | custom-call | tf_op jit(solution)/shard_map/tiles/pallas_call | solution.py:233
  47.9 27.7 %all_to_all.20.recv_ref = bf16[128,40,128]{2,1,0:T(8,128)(2,1)} all-to-all(bf16[128,40,128]{2,1,0:T(8,128)(2,1)} %bitcast.13), channel_id=1, replica_groups=mesh['dp'=128] {'dp'}, dimensions={0} | all-to-all | bytes 2621440 | tf_op jit(solution)/shard_map/all_to_all | solution.py:197
  75.7 4.1 %combine.1 = bf16[128,16,128]{2,1,0:T(8,128)(2,1)} custom-call(s32[256]{0:T(256)} %reshape.38.cols_ref, bf16[128,40,128]{2,1,0:T(8,128)(2,1)} %all_to_all.20.recv_ref), custom_call_target="tpu_custom_call" | custom-call | tf_op jit(solution)/shard_map/combine/pallas_call | solution.py:247
  79.7 19.3 %all_to_all.21.home_ref = bf16[128,16,128]{2,1,0:T(8,128)(2,1)} all-to-all(bf16[128,16,128]{2,1,0:T(8,128)(2,1)} %combine.1), channel_id=1, replica_groups=mesh['dp'=128] {'dp'}, dimensions={0} | all-to-all | bytes 1048576 | tf_op jit(solution)/shard_map/all_to_all | solution.py:197
  99.0 3.5 %final.1 = (f32[128,1024]{1,0:T(8,128)}, f32[128,1024]{1,0:T(8,128)}) custom-call(bf16[128,1024]{1,0:T(8,128)(2,1)} %q_ref.3, bf16[128,1024]{1,0:T(8,128)(2,1)} %d_ref.3, bf16[128,1024]{1,0:T(8,128)(2,1)} %get-tuple-element.10.qu_ref, bf16[128,1024]{1,0:T(8,128)(2,1)} %get-tuple-element.11.du_ref, f32[128,2]{1,0:T(8,128)} %get-tuple-element.12.inv_ref, ...), custom_call_target="tpu_custom_call" | custom-call | tf_op jit(solution)/shard_map/final/pallas_call | solution.py:251
  (3 shorter events, 0.0 us)
Async XLA Ops:
  0.6 22.3 %all-to-all-start = ((bf16[128,8,128]{2,1,0:T(8,128)(2,1)}), bf16[128,8,128]{2,1,0:T(8,128)(2,1)S(1)}, u32[]{:S(2)}, u32[]{:S(2)}) async-start(bf16[128,8,128]{2,1,0:T(8,128)(2,1)} %bitcast.12), calls=%async_computation | async-start | bytes 524288 | tf_op jit(solution)/shard_map/all_to_all | solution.py:197
  22.9 0.7 copy-start.1
  25.7 18.3 %all-to-all-start.1 = ((bf16[128,16,128]{2,1,0:T(8,128)(2,1)}), bf16[128,16,128]{2,1,0:T(8,128)(2,1)S(1)}, u32[]{:S(2)}, u32[]{:S(2)}) async-start(bf16[128,16,128]{2,1,0:T(8,128)(2,1)} %gather.1), calls=%async_computation.1 | async-start | bytes 1048576 | tf_op jit(solution)/shard_map/all_to_all | solution.py:197
  44.0 0.8 copy-start

commit v2 on v1

--- a/solution.py
+++ b/solution.py
@@ -9,6 +9,7 @@
 EPSILON = 1e-06
 LANES = 128
 SUB = 8
+VMEM_BYTES = 16 * 1024 * 1024
 
 
 def whole(space):
@@ -16,14 +17,21 @@
 
 
 def vmem_call(body, outs, n_smem, n_vmem, scratch=(), name=None):
-    return pl.pallas_call(
+    call = pl.pallas_call(
         body,
         out_shape=outs,
         in_specs=[whole(pltpu.SMEM)] * n_smem + [whole(pltpu.VMEM)] * n_vmem,
         out_specs=jax.tree.map(lambda _: whole(pltpu.VMEM), outs),
         scratch_shapes=list(scratch),
+        compiler_params=pltpu.CompilerParams(vmem_limit_bytes=VMEM_BYTES),
         name=name,
     )
+
+    def run(*args):
+        kept = [pltpu.with_memory_space_constraint(x, pltpu.VMEM) for x in args[n_smem:]]
+        return call(*args[:n_smem], *kept)
+
+    return run
 
 
 def inverse_norm(wide):
@@ -213,7 +221,7 @@
     rows, features = query_emb.shape
     row_tiles, col_tiles = rows // SUB, features // LANES
     assert row_tiles * col_tiles == blocks
-    sds = jax.ShapeDtypeStruct
+    sds = pltpu.VMEM
     bf16, f32 = jnp.bfloat16, jnp.float32
 
     doc_pieces = doc_emb.reshape(row_tiles, SUB, col_tiles, LANES).transpose(0, 2, 1, 3)
@@ -249,7 +257,7 @@
     )(cols, parts)
     home = exchange(combined)
     return vmem_call(
-        final_kernel, (sds((rows, features), f32), sds((rows, features), f32)), 0, 10, name="final"
+        final_kernel, (jax.ShapeDtypeStruct((rows, features), f32), jax.ShapeDtypeStruct((rows, features), f32)), 0, 10, name="final"
     )(query_emb, doc_emb, qu, du, inv, et_own, et, row_total, dk, home)
 
 

time: 103 us -> 92.8 us (0.901)
  Pallas kernels: 14.9 us -> 7.22 us
  blocking collectives: 47 us -> 44.4 us
  waiting for transfers between devices: 19.3 us -> 21.5 us
  local copies, waits for them, and re-layouts: 3.65 us -> 1.58 us
    pallas_call x5, Pallas kernels: 14.9 us -> 7.22 us  [run(): return call(*args[:n_smem], *kept)]
    all_to_all x2, blocking collectives: 47 us -> 44.4 us  [exchange(): return lax.all_to_all(x, 'dp', split_axis=0, concat_axis=0, tiled=True)]
    all_to_all x2, waiting for transfers between devices: 19.3 us -> 21.5 us  [exchange(): return lax.all_to_all(x, 'dp', split_axis=0, concat_axis=0, tiled=True)]
    unnamed x4, local copies, waits for them, and re-layouts: 1.49 us -> 0.01 us
  transfers between devices with their start and end apart: 2 -> 2, of which waited for: 2 -> 2; matrix products, arithmetic and copies ran while one was open for 3% -> 3% of each run, Pallas kernels for 2% -> 0%
where the time goes in v2:
time: 92.8 us; the launch traced here: 92.5 us
  blocking collectives  44.4 us (48%)
  waiting for transfers between devices  21.5 us (23%)
  starting transfers between devices  16.2 us (17%)
  Pallas kernels  7.22 us (8%)
  local copies, waits for them, and re-layouts  1.58 us (2%)
    all_to_all x2, blocking collectives, exchange(): return lax.all_to_all(x, 'dp', split_axis=0, concat_axis=0, tiled=True)  44.4 us
    all_to_all x2, waiting for transfers between devices, exchange(): return lax.all_to_all(x, 'dp', split_axis=0, concat_axis=0, tiled=True)  21.5 us
    all_to_all x2, starting transfers between devices, exchange(): return lax.all_to_all(x, 'dp', split_axis=0, concat_axis=0, tiled=True)  16.2 us
    pallas_call x5, Pallas kernels, run(): return call(*args[:n_smem], *kept)  7.22 us
  transfers between devices with their start and end apart: 2, of which 2 were waited for; matrix products, arithmetic and copies ran while one was open for 3% of the time, Pallas kernels for 0%

profile of v2, /device:TPU:1, one launch (start us, length us, event | category | flops | bytes accessed | tf_op | source)
XLA Modules:
  0.0 92.5 jit_solution(11337092565216735208)
XLA Ops:
  0.6 0.0 copy-start
  0.6 0.0 copy-start.1
  0.6 11.5 %all-to-all-start = ((bf16[128,8,128]{2,1,0:T(8,128)(2,1)}), bf16[128,8,128]{2,1,0:T(8,128)(2,1)S(1)}, u32[]{:S(2)}, u32[]{:S(2)}) async-start(bf16[128,8,128]{2,1,0:T(8,128)(2,1)} %bitcast.12), calls=%async_computation | async-start | bytes 524288 | tf_op jit(solution)/shard_map/all_to_all | solution.py:205
  12.1 0.8 fusion
  12.9 0.7 iota_compare_fusion.1
  13.7 0.1 lt.23
  13.8 0.1 copy.9
  13.9 0.1 squeeze.3
  14.0 0.1 copy.10
  14.1 0.1 broadcast_in_dim.28
  14.2 0.1 select_reduce_fusion.1
  14.4 0.1 copy.11
  14.5 0.1 reshape.38.cols_ref
  14.6 8.3 %all-to-all-done.spread_ref = bf16[128,8,128]{2,1,0:T(8,128)(2,1)S(1)} async-done(((bf16[128,8,128]{2,1,0:T(8,128)(2,1)}), bf16[128,8,128]{2,1,0:T(8,128)(2,1)S(1)}, u32[]{:S(2)}, u32[]{:S(2)}) %all-to-all-start) | async-done | bytes 262176 | tf_op jit(solution)/shard_map/all_to_all | solution.py:205
  23.0 1.7 %gather.1 = bf16[128,16,128]{2,1,0:T(8,128)(2,1)} custom-call(s32[256]{0:T(256)S(1)} %reshape.38.cols_ref, bf16[128,8,128]{2,1,0:T(8,128)(2,1)S(1)} %all-to-all-done.spread_ref), custom_call_target="tpu_custom_call" | custom-call | tf_op jit(solution)/shard_map/gather/pallas_call | solution.py:32
  24.6 4.7 %all-to-all-start.1 = ((bf16[128,16,128]{2,1,0:T(8,128)(2,1)}), bf16[128,16,128]{2,1,0:T(8,128)(2,1)S(1)}, u32[]{:S(2)}, u32[]{:S(2)}) async-start(bf16[128,16,128]{2,1,0:T(8,128)(2,1)} %gather.1), calls=%async_computation.1 | async-start | bytes 1048576 | tf_op jit(solution)/shard_map/all_to_all | solution.py:205
  29.4 0.0 copy-done
  29.4 0.4 own.1
  29.8 13.2 %all-to-all-done.1.fetched_ref = bf16[128,16,128]{2,1,0:T(8,128)(2,1)S(1)} async-done(((bf16[128,16,128]{2,1,0:T(8,128)(2,1)}), bf16[128,16,128]{2,1,0:T(8,128)(2,1)S(1)}, u32[]{:S(2)}, u32[]{:S(2)}) %all-to-all-start.1) | async-done | bytes 524320 | tf_op jit(solution)/shard_map/all_to_all | solution.py:205
  42.9 0.9 tiles.1
  43.8 26.5 %all_to_all.20.recv_ref = bf16[128,40,128]{2,1,0:T(8,128)(2,1)S(1)} all-to-all(bf16[128,40,128]{2,1,0:T(8,128)(2,1)S(1)} %bitcast.13), channel_id=1, replica_groups=mesh['dp'=128] {'dp'}, dimensions={0} | all-to-all | bytes 2621440 | tf_op jit(solution)/shard_map/all_to_all | solution.py:205
  70.3 2.3 %combine.1 = bf16[128,16,128]{2,1,0:T(8,128)(2,1)S(1)} custom-call(s32[256]{0:T(256)S(1)} %reshape.38.cols_ref, bf16[128,40,128]{2,1,0:T(8,128)(2,1)S(1)} %all_to_all.20.recv_ref), custom_call_target="tpu_custom_call" | custom-call | tf_op jit(solution)/shard_map/combine/pallas_call | solution.py:32
  72.7 17.9 %all_to_all.21.home_ref = bf16[128,16,128]{2,1,0:T(8,128)(2,1)S(1)} all-to-all(bf16[128,16,128]{2,1,0:T(8,128)(2,1)S(1)} %combine.1), channel_id=1, replica_groups=mesh['dp'=128] {'dp'}, dimensions={0} | all-to-all | bytes 1048576 | tf_op jit(solution)/shard_map/all_to_all | solution.py:205
  90.5 2.0 %final.1 = (f32[128,1024]{1,0:T(8,128)}, f32[128,1024]{1,0:T(8,128)}) custom-call(bf16[128,1024]{1,0:T(8,128)(2,1)S(1)} %copy-done.1, bf16[128,1024]{1,0:T(8,128)(2,1)S(1)} %copy-done, bf16[128,1024]{1,0:T(8,128)(2,1)S(1)} %get-tuple-element.10.qu_ref, bf16[128,1024]{1,0:T(8,128)(2,1)S(1)} %get-tuple-element.11.du_ref, ...), custom_call_target="tpu_custom_call" | custom-call | tf_op jit(solution)/shard_map/final/pallas_call | solution.py:32
  (3 shorter events, 0.0 us)
Async XLA Ops:
  0.6 28.7 %copy-start = (bf16[128,1024]{1,0:T(8,128)(2,1)S(1)}, bf16[128,1024]{1,0:T(8,128)(2,1)}, u32[]{:S(2)}) copy-start(bf16[128,1024]{1,0:T(8,128)(2,1)} %d_ref.3) | copy-start | bytes 786436
  0.6 28.7 %copy-start.1 = (bf16[128,1024]{1,0:T(8,128)(2,1)S(1)}, bf16[128,1024]{1,0:T(8,128)(2,1)}, u32[]{:S(2)}) copy-start(bf16[128,1024]{1,0:T(8,128)(2,1)} %q_ref.3) | copy-start | bytes 786436
  0.6 22.3 %all-to-all-start = ((bf16[128,8,128]{2,1,0:T(8,128)(2,1)}), bf16[128,8,128]{2,1,0:T(8,128)(2,1)S(1)}, u32[]{:S(2)}, u32[]{:S(2)}) async-start(bf16[128,8,128]{2,1,0:T(8,128)(2,1)} %bitcast.12), calls=%async_computation | async-start | bytes 524288 | tf_op jit(solution)/shard_map/all_to_all | solution.py:205
  24.6 18.3 %all-to-all-start.1 = ((bf16[128,16,128]{2,1,0:T(8,128)(2,1)}), bf16[128,16,128]{2,1,0:T(8,128)(2,1)S(1)}, u32[]{:S(2)}, u32[]{:S(2)}) async-start(bf16[128,16,128]{2,1,0:T(8,128)(2,1)} %gather.1), calls=%async_computation.1 | async-start | bytes 1048576 | tf_op jit(solution)/shard_map/all_to_all | solution.py:205

commit v3 on v2

v3 whole, which is shorter than its diff:
```python
import jax
import jax.numpy as jnp
from jax import lax
from jax.experimental import pallas as pl
from jax.experimental.pallas import tpu as pltpu
from jax.sharding import PartitionSpec as P

LOGIT_SCALE = 64.0
EPSILON = 1e-06
LANES = 128
SUB = 8
PIECE = 16
VMEM_BYTES = 16 * 1024 * 1024
BF16 = jnp.bfloat16
F32 = jnp.float32


def vmem_call(body, outs, n_smem, n_vmem, scratch=(), name=None):
    spaces = [pltpu.SMEM] * n_smem + [pltpu.VMEM] * n_vmem
    call = pl.pallas_call(
        body,
        out_shape=outs,
        in_specs=[pl.BlockSpec(memory_space=space) for space in spaces],
        out_specs=jax.tree.map(lambda _: pl.BlockSpec(memory_space=pltpu.VMEM), outs),
        scratch_shapes=list(scratch),
        compiler_params=pltpu.CompilerParams(vmem_limit_bytes=VMEM_BYTES),
        name=name,
    )

    def run(*args):
        kept = [pltpu.with_memory_space_constraint(x, pltpu.VMEM) for x in args[n_smem:]]
        return call(*args[:n_smem], *kept)

    return run


def inverse_norm(wide):
    return lax.rsqrt(jnp.sum(wide * wide, axis=1, keepdims=True) + EPSILON)


def from_pieces(pieces, first):
    row_tiles, pairs = pieces.shape[:2]
    chunks = []
    for pair in range(pairs):
        for half in range(PIECE // SUB):
            at = first + half * SUB
            chunks.append(pieces[:, pair, at : at + SUB].reshape(row_tiles * SUB, LANES))
    return jnp.concatenate(chunks, axis=1)


def dot_nt(a, b):
    return lax.dot_general(a, b, (((1,), (1,)), ((), ())), preferred_element_type=F32)


def dot_tn(a, b):
    return lax.dot_general(a, b, (((0,), (0,)), ((), ())), preferred_element_type=F32)


def dot_nn(a, b):
    return lax.dot_general(a, b, (((1,), (0,)), ((), ())), preferred_element_type=F32)


def own_kernel(q_ref, d_ref, qu_ref, du_ref, inv_ref, et_ref):
    q_wide = q_ref[...].astype(F32)
    d_wide = d_ref[...].astype(F32)
    q_inv = inverse_norm(q_wide)
    d_inv = inverse_norm(d_wide)
    q = (q_wide * q_inv).astype(BF16)
    d = (d_wide * d_inv).astype(BF16)
    qu_ref[...] = q
    du_ref[...] = d
    lane = lax.broadcasted_iota(jnp.int32, inv_ref.shape, 1)
    inv_ref[...] = jnp.where(lane == 0, q_inv, d_inv)
    et_ref[...] = jnp.exp(LOGIT_SCALE * dot_nt(d, q))


def gather_kernel(cols_ref, mine_ref, other_ref, out_ref):
    chips = out_ref.shape[0]

    def step(dest, carry):
        for k in range(2):
            col = cols_ref[2 * dest + k]
            chip = lax.rem(col, chips)
            block = jnp.where(col < chips, mine_ref[chip], other_ref[chip])
            out_ref[dest, k * PIECE : (k + 1) * PIECE, :] = block
        return carry

    lax.fori_loop(0, chips, step, 0, unroll=8)


def split_pair(value, odd):
    high = value.astype(BF16).astype(F32)
    return jnp.where(odd, value - high, high)


def tiles_kernel(qu_ref, et_own_ref, fetched_ref, send_ref, et_ref, row_ref, dk_ref):
    row_tiles, pairs = send_ref.shape[:2]
    q = qu_ref[...]
    pieces = fetched_ref[...].astype(F32).reshape(row_tiles, pairs, 2 * PIECE, LANES)
    et_own = et_own_ref[...]
    row_total = jnp.sum(et_own, axis=0, keepdims=True)
    col_own = jnp.sum(et_own, axis=1, keepdims=True)
    ets, cols = [], []
    for k in range(2):
        wide = from_pieces(pieces, k * PIECE)
        unit = (wide * inverse_norm(wide)).astype(BF16)
        dk_ref[k] = unit
        et = jnp.exp(LOGIT_SCALE * dot_nt(unit, q))
        et_ref[k] = et
        row_total = row_total + jnp.sum(et, axis=0, keepdims=True)
        cols.append(jnp.sum(et, axis=1, keepdims=True))
        ets.append(et)
    row_ref[...] = row_total
    row_inv = 1.0 / row_total
    half = 0.5 * LOGIT_SCALE
    at = 0
    for make in (lambda e: e * row_inv, lambda e: e):
        for et in ets:
            part = half * dot_nn(make(et).astype(BF16), q)
            for pair in range(pairs):
                lanes = pair * 2 * LANES
                both = [
                    part[:, lanes + h * LANES : lanes + (h + 1) * LANES].reshape(row_tiles, 1, SUB, LANES)
                    for h in range(2)
                ]
                both = jnp.concatenate(both, axis=1).reshape(row_tiles, PIECE, LANES)
                send_ref[:, pair, at : at + PIECE, :] = both.astype(BF16)
            at += PIECE
    lane = lax.broadcasted_iota(jnp.int32, (row_tiles * SUB, LANES), 1)
    value = jnp.where(lane < 2, col_own, jnp.where(lane < 4, cols[0], cols[1]))
    scalars = split_pair(value, lane % 2 == 1).reshape(row_tiles, SUB, LANES).astype(BF16)
    for pair in range(pairs):
        send_ref[:, pair, at:, :] = scalars


def add_kernel(cols_ref, recv_ref, swap_ref, acc_a, acc_b, acc_t):
    chips = recv_ref.shape[0]
    acc_a[...] = jnp.zeros_like(acc_a)
    acc_b[...] = jnp.zeros_like(acc_b)
    lane3 = lax.broadcasted_iota(jnp.int32, (chips, SUB, LANES), 2)
    acc_t[0:chips] = jnp.where(lane3 < 2, recv_ref[:, 4 * PIECE :, :].astype(F32), 0.0)
    acc_t[chips:] = jnp.zeros((chips, SUB, LANES), F32)
    lane = lax.broadcasted_iota(jnp.int32, (SUB, LANES), 1)
    masks = [(lane >= 2) & (lane < 4), (lane >= 4) & (lane < 6)]

    def add(source, carry):
        t = recv_ref[source, 4 * PIECE :, :].astype(F32)
        for k in range(2):
            col = cols_ref[2 * source + k]
            a = recv_ref[source, k * PIECE : (k + 1) * PIECE, :].astype(F32)
            b = recv_ref[source, (k + 2) * PIECE : (k + 3) * PIECE, :].astype(F32)
            acc_a[col] = acc_a[col] + a
            acc_b[col] = acc_b[col] + b
            acc_t[col] = acc_t[col] + jnp.where(masks[k], t, 0.0)
        return carry

    lax.fori_loop(0, chips, add, 0, unroll=8)
    total = jnp.broadcast_to(jnp.sum(acc_t[...], axis=2, keepdims=True), acc_t.shape)
    acc_t[...] = total
    swap_ref[:, 0:PIECE, :] = acc_a[chips:].astype(BF16)
    swap_ref[:, PIECE : 2 * PIECE, :] = acc_b[chips:].astype(BF16)
    odd = lax.broadcasted_iota(jnp.int32, total.shape, 2) % 2 == 1
    pair = split_pair(total, odd).astype(BF16)
    swap_ref[:, 2 * PIECE : 2 * PIECE + SUB, :] = pair[chips:]
    swap_ref[:, 2 * PIECE + SUB :, :] = pair[:chips]


def finish_kernel(cols_ref, swap_ref, acc_a, acc_b, acc_t, out_ref, total_ref):
    chips = out_ref.shape[0]
    lane3 = lax.broadcasted_iota(jnp.int32, (chips, SUB, LANES), 2)

    def total_of(at, mine):
        pair = jnp.where(lane3 < 2, swap_ref[:, at : at + SUB, :].astype(F32), 0.0)
        return mine + jnp.broadcast_to(jnp.sum(pair, axis=2, keepdims=True), mine.shape)

    own_total = total_of(2 * PIECE, acc_t[0:chips])
    total_ref[0:chips] = own_total
    total_ref[chips:] = total_of(2 * PIECE + SUB, acc_t[chips:])
    inverse = 1.0 / own_total
    inverse = jnp.concatenate([inverse[:, None], inverse[:, None]], axis=1).reshape(chips, PIECE, LANES)
    a = acc_a[0:chips] + swap_ref[:, 0:PIECE, :].astype(F32)
    b = acc_b[0:chips] + swap_ref[:, PIECE : 2 * PIECE, :].astype(F32)
    out_ref[:, 0:PIECE, :] = (a + b * inverse).astype(BF16)
    lane = lax.broadcasted_iota(jnp.int32, (SUB, LANES), 1)
    odd = lane % 2 == 1

    def emit(dest, carry):
        value = jnp.where(
            lane < 2,
            total_ref[dest],
            jnp.where(lane < 4, total_ref[cols_ref[2 * dest]], total_ref[cols_ref[2 * dest + 1]]),
        )
        out_ref[dest, PIECE:, :] = split_pair(value, odd).astype(BF16)
        return carry

    lax.fori_loop(0, chips, emit, 0, unroll=8)


def unit_grad(wide, inverse, upstream):
    radial = jnp.sum(wide * upstream, axis=1, keepdims=True)
    return upstream * inverse - wide * (radial * inverse * inverse * inverse)


def final_kernel(
    q_ref, d_ref, qu_ref, du_ref, inv_ref, et_own_ref, et_ref, row_ref, dk_ref, home_ref, gq_ref, gd_ref
):
    rows = q_ref.shape[0]
    row_tiles = rows // SUB
    pieces = home_ref[...].astype(F32)
    pieces = pieces.reshape(row_tiles, pieces.shape[0] // row_tiles, PIECE + SUB, LANES)
    scalars = pieces[:, 0, PIECE:].reshape(rows, LANES)
    totals = [scalars[:, 2 * i : 2 * i + 1] + scalars[:, 2 * i + 1 : 2 * i + 2] for i in range(3)]
    row_inv = 1.0 / row_ref[...]

    def weight(et, total):
        return 0.5 * (et * row_inv + et * (1.0 / total))

    own = weight(et_own_ref[...], totals[0])
    diagonal = lax.broadcasted_iota(jnp.int32, own.shape, 0) == lax.broadcasted_iota(
        jnp.int32, own.shape, 1
    )
    own = (own - jnp.where(diagonal, 1.0, 0.0)).astype(BF16)

    def part(x):
        return (LOGIT_SCALE * x).astype(BF16).astype(F32)

    query = part(dot_tn(own, du_ref[...]))
    for k in range(2):
        w = weight(et_ref[k], totals[k + 1]).astype(BF16)
        query = query + part(dot_tn(w, dk_ref[k]))
    gq_ref[...] = unit_grad(q_ref[...].astype(F32), inv_ref[:, 0:1], query)
    doc = part(dot_nn(own, qu_ref[...])) + from_pieces(pieces, 0)
    gd_ref[...] = unit_grad(d_ref[...].astype(F32), inv_ref[:, 1:2], doc)


def row_columns(pair_blocks, active_pair_count, chips, core):
    slots = pair_blocks.shape[1]
    live = jnp.arange(slots)[None, :] < active_pair_count[:, None]
    rows = jnp.where(live, pair_blocks[:, :, 0], -1).reshape(1, -1)
    cols = pair_blocks[:, :, 1].reshape(1, -1)
    match = rows == (2 * jnp.arange(chips) + core)[:, None]
    low = jnp.min(jnp.where(match, cols, 2 * chips - 1), axis=1)
    high = jnp.max(jnp.where(match, cols, 0), axis=1)
    both = jnp.stack([low, high], axis=1).reshape(-1).astype(jnp.int32)
    return (both % 2 != core).astype(jnp.int32) * chips + both // 2


def on_device(query_emb, doc_emb, pair_blocks, active_pair_count):
    blocks = lax.axis_size("dp")
    chips = blocks // 2
    core = lax.axis_index("dp") % 2
    rows, features = query_emb.shape
    row_tiles, pairs = rows // SUB, features // (2 * LANES)
    assert row_tiles * pairs == chips
    groups = [[2 * chip + c for chip in range(chips)] for c in range(2)]

    def exchange(x):
        return lax.all_to_all(x, "dp", 0, 0, tiled=True, axis_index_groups=groups)

    def swap_cores(x):
        return lax.ppermute(x, "dp", [(i, i ^ 1) for i in range(blocks)])

    vmem = pltpu.VMEM
    doc_pieces = doc_emb.reshape(row_tiles, SUB, 2 * pairs, LANES).transpose(0, 2, 1, 3)
    spread = exchange(doc_pieces.reshape(chips, PIECE, LANES))
    cols = row_columns(pair_blocks, active_pair_count, chips, core)
    qu, du, inv, et_own = vmem_call(
        own_kernel,
        (vmem((rows, features), BF16), vmem((rows, features), BF16), vmem((rows, 2), F32), vmem((rows, rows), F32)),
        0,
        2,
        name="own",
    )(query_emb, doc_emb)
    wanted = vmem_call(gather_kernel, vmem((chips, 2 * PIECE, LANES), BF16), 1, 2, name="gather")(
        cols, spread, swap_cores(spread)
    )
    fetched = exchange(wanted)
    send, et, row_total, dk = vmem_call(
        tiles_kernel,
        (
            vmem((row_tiles, pairs, 4 * PIECE + SUB, LANES), BF16),
            vmem((2, rows, rows), F32),
            vmem((1, rows), F32),
            vmem((2, rows, features), BF16),
        ),
        0,
        3,
        name="tiles",
    )(qu, et_own, fetched)
    parts = exchange(send.reshape(chips, 4 * PIECE + SUB, LANES))
    to_other, acc_a, acc_b, acc_t = vmem_call(
        add_kernel,
        (
            vmem((chips, 2 * PIECE + 2 * SUB, LANES), BF16),
            vmem((blocks, PIECE, LANES), F32),
            vmem((blocks, PIECE, LANES), F32),
            vmem((blocks, SUB, LANES), F32),
        ),
        1,
        1,
        name="add",
    )(cols, parts)
    combined = vmem_call(
        finish_kernel,
        vmem((chips, PIECE + SUB, LANES), BF16),
        1,
        4,
        (pltpu.VMEM((blocks, SUB, LANES), F32),),
        name="finish",
    )(cols, swap_cores(to_other), acc_a, acc_b, acc_t)
    home = exchange(combined)
    grad = jax.ShapeDtypeStruct((rows, features), F32)
    return vmem_call(final_kernel, (grad, grad), 0, 10, name="final")(
        query_emb, doc_emb, qu, du, inv, et_own, et, row_total, dk, home
    )


def solution(mesh):
    return jax.shard_map(
        on_device,
        mesh=mesh,
        in_specs=(P("dp", None), P("dp", None), P(), P()),
        out_specs=(P("dp", None), P("dp", None)),
        check_vma=False,
    )
```

time: 92.8 us -> 92.7 us (level)
  blocking collectives: 44.4 us -> 36.7 us
  starting transfers between devices: 16.2 us -> 22.6 us
    all_to_all x2, blocking collectives: 44.4 us -> 36.7 us  [exchange(): return lax.all_to_all(x, 'dp', 0, 0, tiled=True, axis_index_groups=groups)]
    ppermute x0 -> x2, starting transfers between devices: none -> 5.99 us  [swap_cores(): return lax.ppermute(x, 'dp', [(i, i ^ 1) for i in range(blocks)])]
    all_to_all x2, waiting for transfers between devices: 21.5 us -> 18.6 us  [exchange(): return lax.all_to_all(x, 'dp', 0, 0, tiled=True, axis_index_groups=groups)]
    ppermute x0 -> x2, waiting for transfers between devices: none -> 2.81 us  [swap_cores(): return lax.ppermute(x, 'dp', [(i, i ^ 1) for i in range(blocks)])]
    pallas_call x5 -> x6, Pallas kernels: 7.22 us -> 7.64 us  [run(): return call(*args[:n_smem], *kept)]
  transfers between devices with their start and end apart: 2 -> 4, of which waited for: 2 -> 4; matrix products, arithmetic and copies ran while one was open for 3% -> 3% of each run, Pallas kernels for 0% -> 0%
where the time goes in v3:
time: 92.7 us; the launch traced here: 91.7 us
  blocking collectives  36.7 us (40%)
  starting transfers between devices  22.6 us (24%)
  waiting for transfers between devices  21.5 us (23%)
  Pallas kernels  7.64 us (8%)
  local copies, waits for them, and re-layouts  1.57 us (2%)
  other arithmetic  0.96 us (1%)
    all_to_all x2, blocking collectives, exchange(): return lax.all_to_all(x, 'dp', 0, 0, tiled=True, axis_index_groups=groups)  36.7 us
    all_to_all x2, waiting for transfers between devices, exchange(): return lax.all_to_all(x, 'dp', 0, 0, tiled=True, axis_index_groups=groups)  18.6 us
    all_to_all x2, starting transfers between devices, exchange(): return lax.all_to_all(x, 'dp', 0, 0, tiled=True, axis_index_groups=groups)  16.6 us
    pallas_call x6, Pallas kernels, run(): return call(*args[:n_smem], *kept)  7.64 us
    ppermute x2, starting transfers between devices, swap_cores(): return lax.ppermute(x, 'dp', [(i, i ^ 1) for i in range(blocks)])  5.99 us
    ppermute x2, waiting for transfers between devices, swap_cores(): return lax.ppermute(x, 'dp', [(i, i ^ 1) for i in range(blocks)])  2.81 us
  transfers between devices with their start and end apart: 4, of which 4 were waited for; matrix products, arithmetic and copies ran while one was open for 3% of the time, Pallas kernels for 0%

profile of v3, /device:TPU:1, one launch (start us, length us, event | category | flops | bytes accessed | tf_op | source)
XLA Modules:
  0.0 91.7 jit_solution(13801222269842378014)
XLA Ops:
  0.6 12.0 %all-to-all-start = ((bf16[64,16,128]{2,1,0:T(8,128)(2,1)}), bf16[64,16,128]{2,1,0:T(8,128)(2,1)S(1)}, u32[]{:S(2)}, u32[]{:S(2)}) async-start(bf16[64,16,128]{2,1,0:T(8,128)(2,1)} %bitcast.12), calls=%async_computation | async-start | bytes 524288 | tf_op jit(solution)/shard_map/all_to_all | solution.py:258
  12.6 0.8 fusion.3
  13.4 0.7 iota_compare_fusion
  14.1 0.1 lt.35
  14.2 0.1 copy.10
  14.3 0.1 squeeze.3
  14.5 0.1 copy.11
  14.7 0.2 fusion
  14.9 7.0 %all-to-all-done.mine_ref = bf16[64,16,128]{2,1,0:T(8,128)(2,1)S(1)} async-done(((bf16[64,16,128]{2,1,0:T(8,128)(2,1)}), bf16[64,16,128]{2,1,0:T(8,128)(2,1)S(1)}, u32[]{:S(2)}, u32[]{:S(2)}) %all-to-all-start) | async-done | bytes 262176 | tf_op jit(solution)/shard_map/all_to_all | solution.py:258
  22.0 2.2 %collective-permute-start = (bf16[64,16,128]{2,1,0:T(8,128)(2,1)S(1)}, bf16[64,16,128]{2,1,0:T(8,128)(2,1)S(1)}, u32[]{:S(2)}, u32[]{:S(2)}) collective-permute-start(bf16[64,16,128]{2,1,0:T(8,128)(2,1)S(1)} %all-to-all-done.mine_ref), channel_id=1, source_target_pairs={{0,1},{1,0},{2,3},{3,2},{4,5},{5,4},{6,7},{7,6},{8,9},{9,8},{10,11... | collective-permute-start | bytes 786440 | tf_op jit(solution)/shard_map/ppermute | solution.py:261
  24.2 0.1 reshape.43
  24.4 0.9 collective-permute-done.other_ref
  25.3 1.9 %gather.1 = bf16[64,32,128]{2,1,0:T(8,128)(2,1)} custom-call(s32[128]{0:T(128)S(1)} %fusion.2.cols_ref, bf16[64,16,128]{2,1,0:T(8,128)(2,1)S(1)} %all-to-all-done.mine_ref, bf16[64,16,128]{2,1,0:T(8,128)(2,1)S(1)} %collective-permute-done.other_ref), custom_call_target="tpu_custom_call" | custom-call | tf_op jit(solution)/shard_map/gather/pallas_call | solution.py:32
  27.1 4.6 %all-to-all-start.1 = ((bf16[64,32,128]{2,1,0:T(8,128)(2,1)}), bf16[64,32,128]{2,1,0:T(8,128)(2,1)S(1)}, u32[]{:S(2)}, u32[]{:S(2)}) async-start(bf16[64,32,128]{2,1,0:T(8,128)(2,1)} %gather.1), calls=%async_computation.1 | async-start | bytes 1048576 | tf_op jit(solution)/shard_map/all_to_all | solution.py:258
  31.8 0.4 own.1
  32.2 11.6 %all-to-all-done.1.fetched_ref = bf16[64,32,128]{2,1,0:T(8,128)(2,1)S(1)} async-done(((bf16[64,32,128]{2,1,0:T(8,128)(2,1)}), bf16[64,32,128]{2,1,0:T(8,128)(2,1)S(1)}, u32[]{:S(2)}, u32[]{:S(2)}) %all-to-all-start.1) | async-done | bytes 524320 | tf_op jit(solution)/shard_map/all_to_all | solution.py:258
  43.8 0.9 tiles.1
  44.7 21.9 %all_to_all.20.recv_ref = bf16[64,72,128]{2,1,0:T(8,128)(2,1)S(1)} all-to-all(bf16[64,72,128]{2,1,0:T(8,128)(2,1)S(1)} %bitcast.13), channel_id=1, replica_groups={{0,2,4,6,8,10,12,14,16,18,20,22,24,26,28,30,32,34,36,38,40,42,44,46,48,..., dimensions={0} | all-to-all | bytes 2359296 | tf_op jit(solution)/shard_map/all_to_all | solution.py:258
  66.6 1.6 %add.40 = (bf16[64,48,128]{2,1,0:T(8,128)(2,1)S(1)}, f32[128,16,128]{2,1,0:T(8,128)S(1)}, f32[128,16,128]{2,1,0:T(8,128)S(1)}, f32[128,8,128]{2,1,0:T(8,128)S(1)}) custom-call(s32[128]{0:T(128)S(1)} %fusion.2.cols_ref, bf16[64,72,128]{2,1,0:T(8,128)(2,1)S(1)} %all_to_all.20.recv_ref), custom_call_target="tpu_custom_call" | custom-call | tf_op jit(solution)/shard_map/add/pallas_call | solution.py:32
  68.2 3.8 %collective-permute-start.1 = (bf16[64,48,128]{2,1,0:T(8,128)(2,1)S(1)}, bf16[64,48,128]{2,1,0:T(8,128)(2,1)S(1)}, u32[]{:S(2)}, u32[]{:S(2)}) collective-permute-start(bf16[64,48,128]{2,1,0:T(8,128)(2,1)S(1)} %get-tuple-element.22), channel_id=1, source_target_pairs={{0,1},{1,0},{2,3},{3,2},{4,5},{5,4},{6,7},{7,6},{8,9},{9,8},{10,11... | collective-permute-start | bytes 2359304 | tf_op jit(solution)/shard_map/ppermute | solution.py:261
  72.0 1.9 %collective-permute-done.1.swap_ref = bf16[64,48,128]{2,1,0:T(8,128)(2,1)S(1)} collective-permute-done((bf16[64,48,128]{2,1,0:T(8,128)(2,1)S(1)}, bf16[64,48,128]{2,1,0:T(8,128)(2,1)S(1)}, u32[]{:S(2)}, u32[]{:S(2)}) %collective-permute-start.1) | collective-permute-done | bytes 786464 | tf_op jit(solution)/shard_map/ppermute | solution.py:261
  73.9 1.0 %finish.1 = bf16[64,24,128]{2,1,0:T(8,128)(2,1)S(1)} custom-call(s32[128]{0:T(128)S(1)} %fusion.2.cols_ref, bf16[64,48,128]{2,1,0:T(8,128)(2,1)S(1)} %collective-permute-done.1.swap_ref, f32[128,16,128]{2,1,0:T(8,128)S(1)} %get-tuple-element.23.acc_a, f32[128,16,128]{2,1,0:T(8,128)S(1)} %get-tuple-element.24.acc_b, f32[128,8,128]{2,1,0:T(8,128)S(1)} %get-tuple-element.25.acc_t), custom_call_target="tpu_custom_call" | custom-call | tf_op jit(solution)/shard_map/finish/pallas_call | solution.py:32
  74.9 14.8 %all_to_all.21.home_ref = bf16[64,24,128]{2,1,0:T(8,128)(2,1)S(1)} all-to-all(bf16[64,24,128]{2,1,0:T(8,128)(2,1)S(1)} %finish.1), channel_id=1, replica_groups={{0,2,4,6,8,10,12,14,16,18,20,22,24,26,28,30,32,34,36,38,40,42,44,46,48,..., dimensions={0} | all-to-all | bytes 786432 | tf_op jit(solution)/shard_map/all_to_all | solution.py:258
  89.8 1.9 %final.1 = (f32[128,1024]{1,0:T(8,128)}, f32[128,1024]{1,0:T(8,128)}) custom-call(bf16[128,1024]{1,0:T(8,128)(2,1)S(1)} %copy-done.1, bf16[128,1024]{1,0:T(8,128)(2,1)S(1)} %copy-done, bf16[128,1024]{1,0:T(8,128)(2,1)S(1)} %get-tuple-element.14.qu_ref, bf16[128,1024]{1,0:T(8,128)(2,1)S(1)} %get-tuple-element.15.du_ref, ...), custom_call_target="tpu_custom_call" | custom-call | tf_op jit(solution)/shard_map/final/pallas_call | solution.py:32
  (10 shorter events, 0.2 us)
Async XLA Ops:
  0.6 21.3 %all-to-all-start = ((bf16[64,16,128]{2,1,0:T(8,128)(2,1)}), bf16[64,16,128]{2,1,0:T(8,128)(2,1)S(1)}, u32[]{:S(2)}, u32[]{:S(2)}) async-start(bf16[64,16,128]{2,1,0:T(8,128)(2,1)} %bitcast.12), calls=%async_computation | async-start | bytes 524288 | tf_op jit(solution)/shard_map/all_to_all | solution.py:258
  14.5 17.3 %copy-start = (bf16[128,1024]{1,0:T(8,128)(2,1)S(1)}, bf16[128,1024]{1,0:T(8,128)(2,1)}, u32[]{:S(2)}) copy-start(bf16[128,1024]{1,0:T(8,128)(2,1)} %d_ref.3) | copy-start | bytes 786436
  14.5 17.3 %copy-start.1 = (bf16[128,1024]{1,0:T(8,128)(2,1)S(1)}, bf16[128,1024]{1,0:T(8,128)(2,1)}, u32[]{:S(2)}) copy-start(bf16[128,1024]{1,0:T(8,128)(2,1)} %q_ref.3) | copy-start | bytes 786436
  22.0 3.3 %collective-permute-start = (bf16[64,16,128]{2,1,0:T(8,128)(2,1)S(1)}, bf16[64,16,128]{2,1,0:T(8,128)(2,1)S(1)}, u32[]{:S(2)}, u32[]{:S(2)}) collective-permute-start(bf16[64,16,128]{2,1,0:T(8,128)(2,1)S(1)} %all-to-all-done.mine_ref), channel_id=1, source_target_pairs={{0,1},{1,0},{2,3},{3,2},{4,5},{5,4},{6,7},{7,6},{8,9},{9,8},{10,11... | collective-permute-start | bytes 786440 | tf_op jit(solution)/shard_map/ppermute | solution.py:261
  27.1 16.7 %all-to-all-start.1 = ((bf16[64,32,128]{2,1,0:T(8,128)(2,1)}), bf16[64,32,128]{2,1,0:T(8,128)(2,1)S(1)}, u32[]{:S(2)}, u32[]{:S(2)}) async-start(bf16[64,32,128]{2,1,0:T(8,128)(2,1)} %gather.1), calls=%async_computation.1 | async-start | bytes 1048576 | tf_op jit(solution)/shard_map/all_to_all | solution.py:258
  68.2 5.7 %collective-permute-start.1 = (bf16[64,48,128]{2,1,0:T(8,128)(2,1)S(1)}, bf16[64,48,128]{2,1,0:T(8,128)(2,1)S(1)}, u32[]{:S(2)}, u32[]{:S(2)}) collective-permute-start(bf16[64,48,128]{2,1,0:T(8,128)(2,1)S(1)} %get-tuple-element.22), channel_id=1, source_target_pairs={{0,1},{1,0},{2,3},{3,2},{4,5},{5,4},{6,7},{7,6},{8,9},{9,8},{10,11... | collective-permute-start | bytes 2359304 | tf_op jit(solution)/shard_map/ppermute | solution.py:261

commit v4 on v2

--- a/solution.py
+++ b/solution.py
@@ -1,3 +1,5 @@
+import functools
+
 import jax
 import jax.numpy as jnp
 from jax import lax
@@ -9,6 +11,9 @@
 EPSILON = 1e-06
 LANES = 128
 SUB = 8
+SHARED = 6
+PICKS = 16
+CHOICES = (4, 5, 6)
 VMEM_BYTES = 16 * 1024 * 1024
 
 
@@ -16,20 +21,22 @@
     return pl.BlockSpec(memory_space=space)
 
 
-def vmem_call(body, outs, n_smem, n_vmem, scratch=(), name=None):
+def vmem_call(body, outs, n_smem, n_vmem, scratch=(), name=None, n_any=0, out_space=pltpu.VMEM, keep=True):
     call = pl.pallas_call(
         body,
         out_shape=outs,
-        in_specs=[whole(pltpu.SMEM)] * n_smem + [whole(pltpu.VMEM)] * n_vmem,
-        out_specs=jax.tree.map(lambda _: whole(pltpu.VMEM), outs),
+        in_specs=[whole(pltpu.SMEM)] * n_smem + [whole(pl.ANY)] * n_any + [whole(pltpu.VMEM)] * n_vmem,
+        out_specs=jax.tree.map(lambda _: whole(out_space), outs),
         scratch_shapes=list(scratch),
         compiler_params=pltpu.CompilerParams(vmem_limit_bytes=VMEM_BYTES),
         name=name,
     )
 
     def run(*args):
-        kept = [pltpu.with_memory_space_constraint(x, pltpu.VMEM) for x in args[n_smem:]]
-        return call(*args[:n_smem], *kept)
+        if not keep:
+            return call(*args)
+        kept = [pltpu.with_memory_space_constraint(x, pltpu.VMEM) for x in args[n_smem + n_any :]]
+        return call(*args[: n_smem + n_any], *kept)
 
     return run
 
@@ -71,17 +78,6 @@
     et_ref[...] = jnp.exp(LOGIT_SCALE * dot_nt(d, q))
 
 
-def gather_kernel(cols_ref, spread_ref, out_ref):
-    def step(dest, carry):
-        first = spread_ref[cols_ref[2 * dest]]
-        second = spread_ref[cols_ref[2 * dest + 1]]
-        out_ref[dest, 0:SUB, :] = first
-        out_ref[dest, SUB : 2 * SUB, :] = second
-        return carry
-
-    lax.fori_loop(0, out_ref.shape[0], step, 0, unroll=8)
-
-
 def split_pair(value, odd):
     high = value.astype(jnp.bfloat16).astype(jnp.float32)
     return jnp.where(odd, value - high, high)
@@ -90,7 +86,7 @@
 def tiles_kernel(qu_ref, et_own_ref, fetched_ref, send_ref, et_ref, row_ref, dk_ref):
     row_tiles, col_tiles = send_ref.shape[:2]
     q = qu_ref[...]
-    pieces = fetched_ref[...].astype(jnp.float32)
+    pieces = fetched_ref[:, 0 : 2 * SUB, :].astype(jnp.float32)
     pieces = pieces.reshape(row_tiles, col_tiles, 2, SUB, LANES)
     et_own = et_own_ref[...]
     row_total = jnp.sum(et_own, axis=0, keepdims=True)
@@ -201,6 +197,154 @@
     gd_ref[...] = unit_grad(d_ref[...].astype(jnp.float32), inv_ref[:, 1:2], doc)
 
 
+def first_gather_kernel(cols_ref, spread_ref, query_ref, out_ref):
+    def step(dest, carry):
+        tiles = [spread_ref[cols_ref[2 * dest + k]] for k in range(2)] + [query_ref[dest]]
+        for slot, tile in enumerate(tiles):
+            out_ref[dest, slot * SUB : (slot + 1) * SUB, :] = tile
+        return carry
+
+    lax.fori_loop(0, out_ref.shape[0], step, 0, unroll=8)
+
+
+def eye_mask(n):
+    return lax.broadcasted_iota(jnp.int32, (n, n), 0) == lax.broadcasted_iota(jnp.int32, (n, n), 1)
+
+
+def to_lanes(column, eye):
+    return jnp.sum(jnp.where(eye, column, 0.0), axis=0, keepdims=True)
+
+
+def to_sublanes(row, eye):
+    return jnp.sum(jnp.where(eye, row, 0.0), axis=1, keepdims=True)
+
+
+def own_pair_kernel(q_ref, d_ref, qu_ref, du_ref, inv_ref, e_ref, et_ref):
+    own_kernel(q_ref, d_ref, qu_ref, du_ref, inv_ref, et_ref)
+    e_ref[...] = jnp.exp(LOGIT_SCALE * dot_nt(qu_ref[...], du_ref[...]))
+
+
+def fetched_rows(fetched_ref, slot, row_tiles, col_tiles):
+    piece = fetched_ref[:, slot * SUB : (slot + 1) * SUB, :].astype(jnp.float32)
+    return from_pieces(piece.reshape(row_tiles, col_tiles, 1, SUB, LANES), 0)
+
+
+def row_side_kernel(
+    table_ref, qu_ref, du_ref, e_own_ref, et_own_ref, fetched_ref, send_ref, e_ref, row_ref, units_ref, extra_ref
+):
+    rows, features = qu_ref.shape
+    row_tiles, col_tiles = rows // SUB, features // LANES
+    shared = send_ref.shape[1] // SUB - 1
+    stride = table_ref.shape[0] // send_ref.shape[0]
+    eye = eye_mask(rows)
+    q = qu_ref[...]
+    units_ref[0:rows] = du_ref[...]
+    row_total = jnp.sum(e_own_ref[...], axis=1, keepdims=True)
+    columns = [to_lanes(jnp.sum(et_own_ref[...], axis=1, keepdims=True), eye)]
+    for k in range(2):
+        wide = fetched_rows(fetched_ref, k, row_tiles, col_tiles)
+        unit = (wide * inverse_norm(wide)).astype(jnp.bfloat16)
+        units_ref[(k + 1) * rows : (k + 2) * rows] = unit
+        e = jnp.exp(LOGIT_SCALE * dot_nt(q, unit))
+        e_ref[k] = e
+        row_total = row_total + jnp.sum(e, axis=1, keepdims=True)
+        columns.append(jnp.sum(e, axis=0, keepdims=True))
+    row_ref[...] = row_total
+    doubled = []
+    for x in [to_lanes(row_total, eye)] + columns:
+        high = x.astype(jnp.bfloat16).astype(jnp.float32)
+        doubled += [high, x - high]
+    extra_ref[...] = jnp.concatenate(doubled, axis=0).astype(jnp.bfloat16)
+    send_ref[:, shared * SUB :, :] = jnp.broadcast_to(extra_ref[...][None], (send_ref.shape[0], SUB, LANES))
+
+    def step(dest, carry):
+        tiles = [
+            fetched_ref[table_ref[dest * stride + slot], 2 * SUB : 3 * SUB, :] for slot in range(shared)
+        ]
+        for slot, tile in enumerate(tiles):
+            send_ref[dest, slot * SUB : (slot + 1) * SUB, :] = tile
+        return carry
+
+    lax.fori_loop(0, send_ref.shape[0], step, 0, unroll=4)
+
+
+def doc_side_kernel(
+    info_ref, other_any, pick_ref, qu_ref, du_ref, et_own_ref, recv_ref,
+    acc_ref, partner_ref, sums_ref, units_ref, other_ref, sem
+):
+    bring = pltpu.make_async_copy(other_any, other_ref, sem)
+    bring.start()
+    rows, features = qu_ref.shape
+    row_tiles, col_tiles = rows // SUB, features // LANES
+    blocks = recv_ref.shape[0]
+    shared = recv_ref.shape[1] // SUB - 1
+    eye = eye_mask(rows)
+    messages = recv_ref[:, shared * SUB :, :].astype(jnp.float32).reshape(blocks * SUB, LANES)
+    sums = dot_nn(pick_ref[...], messages.astype(jnp.bfloat16))
+    sums_ref[...] = sums
+    inverse = [1.0 / to_sublanes(sums[i : i + 1], eye) for i in range(2)]
+
+    def weight(et, row_total, col_inverse):
+        return 0.5 * (et * (1.0 / row_total) + et * col_inverse)
+
+    q = qu_ref[...]
+    own = weight(et_own_ref[...], sums[4:5], inverse[0]) - jnp.where(eye, 1.0, 0.0)
+    units_ref[0:rows] = q
+    weights = [[own.astype(jnp.bfloat16)], [jnp.zeros((rows, rows), jnp.bfloat16)]]
+    bring.wait()
+    for slot in range(shared):
+        entry = info_ref[slot]
+        side = 1 - lax.rem(entry, 2)
+        unit = fetched_rows(recv_ref, slot, row_tiles, col_tiles).astype(jnp.bfloat16)
+        units_ref[(slot + 1) * rows : (slot + 2) * rows] = unit
+        docs = jnp.where(side == 1, other_ref[...], du_ref[...])
+        et = jnp.exp(LOGIT_SCALE * dot_nt(docs, unit))
+        live = entry > 0
+        total = jnp.where(live, sums[5 + slot : 6 + slot], 1.0)
+        w = weight(et, total, jnp.where(side == 1, inverse[1], inverse[0]))
+        for i in range(2):
+            weights[i].append(jnp.where(live & (side == i), w, 0.0).astype(jnp.bfloat16))
+    weights = jnp.concatenate([jnp.concatenate(w, axis=1) for w in weights], axis=0)
+    grads = LOGIT_SCALE * dot_nn(weights, units_ref[...])
+    acc_ref[...] = grads[0:rows]
+    partner_ref[...] = grads[rows:].astype(jnp.bfloat16)
+
+
+def query_side_kernel(sums_ref, q_ref, inv_ref, e_own_ref, e_ref, row_ref, units_ref, gq_ref, buf, sems):
+    eye = eye_mask(q_ref.shape[0])
+    row_inv = 1.0 / row_ref[...]
+
+    def weight(e, which):
+        return 0.5 * (e * row_inv + e * (1.0 / sums_ref[which : which + 1, :]))
+
+    weights = [weight(e_own_ref[...], 0) - jnp.where(eye, 1.0, 0.0)]
+    weights += [weight(e_ref[k], 2 + k) for k in range(2)]
+    query = LOGIT_SCALE * dot_nn(jnp.concatenate(weights, axis=1).astype(jnp.bfloat16), units_ref[...])
+    write_grad(gq_ref, buf, sems, lambda some: (q_ref[some], inv_ref[some, 0:1], query[some]))
+
+
+def write_grad(out_ref, buf, sems, rows_of):
+    parts = sems.shape[0]
+    step = buf.shape[0] // parts
+    copies = []
+    for j in range(parts):
+        some = slice(j * step, (j + 1) * step)
+        raw, inverse, upstream = rows_of(some)
+        buf[some] = unit_grad(raw.astype(jnp.float32), inverse, upstream)
+        at = pl.ds(j * step, step)
+        copies.append(pltpu.make_async_copy(buf.at[at], out_ref.at[at], sems.at[j]))
+        copies[-1].start()
+    for copy in copies:
+        copy.wait()
+
+
+def doc_final_kernel(d_ref, inv_ref, acc_ref, swapped_ref, gd_ref, buf, sems):
+    def rows_of(some):
+        return d_ref[some], inv_ref[some, 1:2], acc_ref[some] + swapped_ref[some].astype(jnp.float32)
+
+    write_grad(gd_ref, buf, sems, rows_of)
+
+
 def exchange(x):
     return lax.all_to_all(x, "dp", split_axis=0, concat_axis=0, tiled=True)
 
@@ -216,28 +360,58 @@
     return jnp.stack([low, high], axis=1).reshape(-1).astype(jnp.int32)
 
 
-def on_device(query_emb, doc_emb, pair_blocks, active_pair_count):
+def shared_slots(cols, blocks):
+    tiles = jnp.arange(cols.shape[0])
+    chip = cols // 2
+    before = (chip[:, None] == chip[None, :]) & (tiles[None, :] < tiles[:, None])
+    rank = jnp.sum(before.astype(jnp.int32), axis=1)
+    device = 2 * chip + rank % 2
+    slot = rank // 2
+    entry = 1 + 2 * (tiles // 2) + (cols % 2 != rank % 2).astype(jnp.int32)
+    place = device * SHARED + slot
+    hit = (place[None, :] == jnp.arange(blocks * SHARED)[:, None]) & (slot[None, :] < SHARED)
+    table = jnp.sum(jnp.where(hit, entry[None, :], 0), axis=1).astype(jnp.int32)
+    return table.reshape(blocks, SHARED), jnp.max(rank)
+
+
+def message_picks(cols, mine, me, blocks):
+    source = jnp.arange(blocks * SUB) // SUB
+    kind = (jnp.arange(blocks * SUB) % SUB) // 2
+    pair = cols.reshape(blocks, 2)
+    own_pair = lax.dynamic_index_in_dim(pair, me, 0, keepdims=False)
+    columns = jnp.concatenate([jnp.stack([me, me ^ 1]).astype(jnp.int32), own_pair])[:, None]
+    first = jnp.repeat(pair[:, 0], SUB)
+    second = jnp.repeat(pair[:, 1], SUB)
+    named = jnp.where(kind == 1, source, jnp.where(kind == 2, first, second))
+    column_hit = (named[None, :] == columns) & (kind > 0)[None, :]
+    row_blocks = jnp.concatenate([me.reshape(1).astype(jnp.int32), (mine + 1) // 2 - 1])[:, None]
+    row_hit = (source[None, :] == row_blocks) & (kind == 0)[None, :]
+    hits = jnp.concatenate([column_hit, row_hit], axis=0).astype(jnp.bfloat16)
+    return jnp.pad(hits, ((0, PICKS - hits.shape[0]), (0, 0)))
+
+
+def pieces(x):
+    rows, features = x.shape
+    tiled = x.reshape(rows // SUB, SUB, features // LANES, LANES).transpose(0, 2, 1, 3)
+    return tiled.reshape(-1, SUB, LANES)
+
+
+def fetch(cols, spread, query_unit):
+    blocks = lax.axis_size("dp")
+    wanted = vmem_call(
+        first_gather_kernel, pltpu.VMEM((blocks, 3 * SUB, LANES), jnp.bfloat16), 1, 2, name="gather"
+    )(cols, spread, pieces(query_unit))
+    return exchange(wanted)
+
+
+def general_path(query_emb, doc_emb, spread, cols, table, info, picks, own):
+    qu, du, inv, _, et_own, _ = own
+    fetched = fetch(cols, spread, qu)
     blocks = lax.axis_size("dp")
     rows, features = query_emb.shape
     row_tiles, col_tiles = rows // SUB, features // LANES
-    assert row_tiles * col_tiles == blocks
     sds = pltpu.VMEM
     bf16, f32 = jnp.bfloat16, jnp.float32
-
-    doc_pieces = doc_emb.reshape(row_tiles, SUB, col_tiles, LANES).transpose(0, 2, 1, 3)
-    spread = exchange(doc_pieces.reshape(blocks, SUB, LANES))
-    cols = row_columns(pair_blocks, active_pair_count, blocks)
-    qu, du, inv, et_own = vmem_call(
-        own_kernel,
-        (sds((rows, features), bf16), sds((rows, features), bf16), sds((rows, 2), f32), sds((rows, rows), f32)),
-        0,
-        2,
-        name="own",
-    )(query_emb, doc_emb)
-    wanted = vmem_call(gather_kernel, sds((blocks, 2 * SUB, LANES), bf16), 1, 1, name="gather")(
-        cols, spread
-    )
-    fetched = exchange(wanted)
     send, et, row_total, dk = vmem_call(
         tiles_kernel,
         (
@@ -256,9 +430,89 @@
         combine_kernel, sds((blocks, 2 * SUB, LANES), bf16), 1, 1, (acc, acc, acc), name="combine"
     )(cols, parts)
     home = exchange(combined)
-    return vmem_call(
-        final_kernel, (jax.ShapeDtypeStruct((rows, features), f32), jax.ShapeDtypeStruct((rows, features), f32)), 0, 10, name="final"
-    )(query_emb, doc_emb, qu, du, inv, et_own, et, row_total, dk, home)
+    grad = jax.ShapeDtypeStruct((rows, features), f32)
+    return vmem_call(final_kernel, (grad, grad), 0, 10, name="final")(
+        query_emb, doc_emb, qu, du, inv, et_own, et, row_total, dk, home
+    )
+
+
+def short_path(shared, query_emb, doc_emb, spread, cols, table, info, picks, own):
+    qu, du, inv, e_own, et_own, other = own
+    fetched = fetch(cols, spread, qu)
+    blocks = lax.axis_size("dp")
+    rows, features = query_emb.shape
+    assert rows == LANES
+    sds = pltpu.VMEM
+    bf16, f32 = jnp.bfloat16, jnp.float32
+    wide = sds((rows, features), bf16)
+    grad = jax.ShapeDtypeStruct((rows, features), f32)
+    send, e, row_total, doc_units = vmem_call(
+        row_side_kernel,
+        (
+            sds((blocks, (shared + 1) * SUB, LANES), bf16),
+            sds((2, rows, rows), f32),
+            sds((rows, 1), f32),
+            sds((3 * rows, features), bf16),
+        ),
+        1,
+        5,
+        (pltpu.VMEM((SUB, LANES), bf16),),
+        name="rows",
+    )(table, qu, du, e_own, et_own, fetched)
+    recv = exchange(send)
+    acc, partner, sums = vmem_call(
+        doc_side_kernel,
+        (sds((rows, features), f32), wide, sds((PICKS, LANES), f32)),
+        1,
+        5,
+        (
+            pltpu.VMEM(((shared + 1) * rows, features), bf16),
+            pltpu.VMEM((rows, features), bf16),
+            pltpu.SemaphoreType.DMA,
+        ),
+        name="docs",
+        n_any=1,
+    )(info, other, picks, qu, du, et_own, recv)
+    swapped = swap_cores(partner)
+    grad_scratch = (pltpu.VMEM((rows, features), f32), pltpu.SemaphoreType.DMA((4,)))
+    grad_query = vmem_call(
+        query_side_kernel, grad, 0, 7, grad_scratch, name="queries", out_space=pl.ANY
+    )(sums, query_emb, inv, e_own, e, row_total, doc_units)
+    grad_doc = vmem_call(
+        doc_final_kernel, grad, 0, 4, grad_scratch, name="final", out_space=pl.ANY
+    )(doc_emb, inv, acc, swapped)
+    return grad_query, grad_doc
+
+
+def swap_cores(x):
+    return lax.ppermute(x, "dp", [(i, i ^ 1) for i in range(lax.axis_size("dp"))])
+
+
+def on_device(query_emb, doc_emb, pair_blocks, active_pair_count):
+    blocks = lax.axis_size("dp")
+    me = lax.axis_index("dp")
+    rows, features = query_emb.shape
+    row_tiles, col_tiles = rows // SUB, features // LANES
+    assert row_tiles * col_tiles == blocks
+
+    spread = exchange(pieces(doc_emb))
+    cols = row_columns(pair_blocks, active_pair_count, blocks)
+    mat, wide = pltpu.VMEM((rows, rows), jnp.float32), pltpu.VMEM((rows, features), jnp.bfloat16)
+    own = vmem_call(
+        own_pair_kernel, (wide, wide, pltpu.VMEM((rows, 2), jnp.float32), mat, mat), 0, 2, name="own", keep=False
+    )(query_emb, doc_emb)
+    own = (*own, swap_cores(own[1]))
+    table, deepest = shared_slots(cols, blocks)
+    info = lax.dynamic_index_in_dim(table, me, 0, keepdims=False)
+    picks = message_picks(cols, info, me, blocks)
+    table = (jnp.maximum(table - 1, 0) // 2).reshape(-1)
+    choice = sum((deepest >= 2 * shared).astype(jnp.int32) for shared in CHOICES)
+    spread, cols, table, info, picks, choice, own = lax.optimization_barrier(
+        (spread, cols, table, info, picks, choice, own)
+    )
+    args = (query_emb, doc_emb, spread, cols, table, info, picks, own)
+    paths = [functools.partial(short_path, shared) for shared in CHOICES] + [general_path]
+    return lax.switch(choice, paths, *args)
 
 
 def solution(mesh):

time: 92.8 us -> 85.1 us (0.917)
  waiting for transfers between devices: 21.5 us -> 1.52 us
  blocking collectives: 44.4 us -> 52.8 us
  starting transfers between devices: 16.2 us -> 13.9 us
  between operations: 0.74 us -> 2.92 us
  Pallas kernels: 7.22 us -> 8.72 us
  other arithmetic: 0.89 us -> 2.36 us
    all_to_all x2 -> x1, waiting for transfers between devices: 21.5 us -> 1.51 us  [exchange(): return lax.all_to_all(x, 'dp', split_axis=0, concat_axis=0, tiled=True)]
    all_to_all x2, blocking collectives: 44.4 us -> 52.8 us  [exchange(): return lax.all_to_all(x, 'dp', split_axis=0, concat_axis=0, tiled=True)]
    all_to_all x2 -> x1, starting transfers between devices: 16.2 us -> 11.5 us  [exchange(): return lax.all_to_all(x, 'dp', split_axis=0, concat_axis=0, tiled=True)]
    ppermute x0 -> x2, starting transfers between devices: none -> 2.46 us  [swap_cores(): lax.ppermute(x, 'dp', [(i, i ^ 1) for i in range(lax.axis_size('dp'))])]
    pallas_call x5 -> x6, Pallas kernels: 7.22 us -> 8.72 us  [the longest x5 7.23 us: run(): return call(*args[:n_smem + n_any], *kept)]
  transfers between devices with their start and end apart: 2 -> 3, of which waited for: 2 -> 1; matrix products, arithmetic and copies ran while one was open for 3% -> 5% of each run, Pallas kernels for 0% -> 3%
where the time goes in v4:
time: 85.1 us; the launch traced here: 84.8 us
  blocking collectives  52.8 us (62%)
  starting transfers between devices  13.9 us (16%)
  Pallas kernels  8.72 us (10%)
  between operations  2.92 us (3%)
  other arithmetic  2.36 us (3%)
  local copies, waits for them, and re-layouts  2.24 us (3%)
  waiting for transfers between devices  1.52 us (2%)
    all_to_all x2, blocking collectives, exchange(): return lax.all_to_all(x, 'dp', split_axis=0, concat_axis=0, tiled=True)  52.8 us
    all_to_all x1, starting transfers between devices, exchange(): return lax.all_to_all(x, 'dp', split_axis=0, concat_axis=0, tiled=True)  11.5 us
    pallas_call x5, Pallas kernels, run(): return call(*args[:n_smem + n_any], *kept)  7.23 us
    ppermute x2, starting transfers between devices, swap_cores(): lax.ppermute(x, 'dp', [(i, i ^ 1) for i in range(lax.axis_size('dp'))])  2.46 us
  transfers between devices with their start and end apart: 3, of which 1 were waited for; matrix products, arithmetic and copies ran while one was open for 5% of the time, Pallas kernels for 3%

profile of v4, /device:TPU:1, one launch (start us, length us, event | category | flops | bytes accessed | tf_op | source)
XLA Modules:
  0.0 84.8 jit_solution(6843632157241077170)
XLA Ops:
  0.6 11.5 %all-to-all-start.9 = ((bf16[128,8,128]{2,1,0:T(8,128)(2,1)}), bf16[128,8,128]{2,1,0:T(8,128)(2,1)S(1)}, u32[]{:S(2)}, u32[]{:S(2)}) async-start(bf16[128,8,128]{2,1,0:T(8,128)(2,1)} %bitcast.41), calls=%async_computation.9 | async-start | bytes 524288 | tf_op jit(solution)/shard_map/all_to_all | solution.py:349
  12.1 1.5 %own.1 = (bf16[128,1024]{1,0:T(8,128)(2,1)S(1)}, bf16[128,1024]{1,0:T(8,128)(2,1)S(1)}, f32[128,2]{1,0:T(8,128)S(1)}, f32[128,128]{1,0:T(8,128)S(1)}, f32[128,128]{1,0:T(8,128)S(1)}) custom-call(bf16[128,1024]{1,0:T(8,128)(2,1)} %q_ref.1, bf16[128,1024]{1,0:T(8,128)(2,1)} %d_ref.1), custom_call_target="tpu_custom_call" | custom-call | tf_op jit(solution)/shard_map/own/pallas_call | solution.py:37
  13.6 1.1 %collective-permute-start.3 = (bf16[128,1024]{1,0:T(8,128)(2,1)S(1)}, bf16[128,1024]{1,0:T(8,128)(2,1)S(1)}, u32[]{:S(2)}, u32[]{:S(2)}) collective-permute-start(bf16[128,1024]{1,0:T(8,128)(2,1)S(1)} %get-tuple-element.195), channel_id=1, source_target_pairs={{0,1},{1,0},{2,3},{3,2},{4,5},{5,4},{6,7},{7,6},{8,9},{9,8},{10,11... | collective-permute-start | bytes 786440 | tf_op jit(solution)/shard_map/ppermute | solution.py:488
  14.8 0.8 fusion.15
  15.6 0.7 iota_compare_fusion.3
  16.3 0.1 lt.75
  16.5 0.1 copy.17
  16.9 0.1 select_reduce_fusion.2
  17.2 0.2 dynamic-slice_reduce_fusion
  17.4 0.1 reshape.276
  17.5 0.2 convert_reduce_fusion
  17.7 0.6 fusion.16
  18.4 0.2 select_reduce_fusion
  18.6 0.1 reshape.277
  21.4 1.5 %all-to-all-done.9 = bf16[128,8,128]{2,1,0:T(8,128)(2,1)S(1)} async-done(((bf16[128,8,128]{2,1,0:T(8,128)(2,1)}), bf16[128,8,128]{2,1,0:T(8,128)(2,1)S(1)}, u32[]{:S(2)}, u32[]{:S(2)}) %all-to-all-start.9) | async-done | bytes 262176 | tf_op jit(solution)/shard_map/all_to_all | solution.py:349
  23.0 61.6 %conditional.1 = ((f32[128,1024]{1,0:T(8,128)}, f32[128,1024]{1,0:T(8,128)})) conditional(s32[]{:T(128)} %clamp.3, (bf16[128,1024]{1,0:T(8,128)(2,1)S(1)}, s32[256]{0:T(256)S(1)}, bf16[128,8,128]{2,1,0:T(8,128)(2,1)S(1)}, s32[768]{0:T(1024)S(1)}, bf16[128,1024]{1,0:T(8,128)(2,1)S(1)}, ...), branch_computations={%region_5.6_spmd, %region_6.7_spmd, %region_7.8_spmd, %region_8.9_... | conditional | bytes 6291520 | solution.py:515
  23.0 0.9 %gather.5 = bf16[128,24,128]{2,1,0:T(8,128)(2,1)S(1)} custom-call(s32[256]{0:T(256)S(1)} %get-tuple-element.122.cols_ref, bf16[128,8,128]{2,1,0:T(8,128)(2,1)S(1)} %get-tuple-element.123.spread_ref, bf16[128,8,128]{2,1,0:T(8,128)(2,1)S(1)} %bitcast.38), custom_call_target="tpu_custom_call" | custom-call | tf_op jit(solution)/shard_map/cond/branch_1_fun/gather/pallas_call | solution.py:39
  23.9 23.5 %all_to_all.43.fetched_ref = bf16[128,24,128]{2,1,0:T(8,128)(2,1)S(1)} all-to-all(bf16[128,24,128]{2,1,0:T(8,128)(2,1)S(1)} %gather.5), channel_id=1, replica_groups=mesh['dp'=128] {'dp'}, dimensions={0} | all-to-all | bytes 1572864 | tf_op jit(solution)/shard_map/cond/branch_1_fun/all_to_all | solution.py:349
  47.4 2.1 %rows.4 = (bf16[128,48,128]{2,1,0:T(8,128)(2,1)S(1)}, f32[2,128,128]{2,1,0:T(8,128)S(1)}, f32[128,1]{1,0:T(8,128)S(1)}, bf16[384,1024]{1,0:T(8,128)(2,1)S(1)}) custom-call(s32[768]{0:T(1024)S(1)} %get-tuple-element.120.table_ref, bf16[128,1024]{1,0:T(8,128)(2,1)S(1)} %get-tuple-element.117.qu_ref, bf16[128,1024]{1,0:T(8,128)(2,1)S(1)} %get-tuple-element.118.du_ref, ...), custom_call_target="tpu_custom_call" | custom-call | tf_op jit(solution)/shard_map/cond/branch_1_fun/rows/pallas_call | solution.py:39
  49.5 29.2 %all_to_all.44.recv_ref = bf16[128,48,128]{2,1,0:T(8,128)(2,1)S(1)} all-to-all(bf16[128,48,128]{2,1,0:T(8,128)(2,1)S(1)} %get-tuple-element.124), channel_id=1, replica_groups=mesh['dp'=128] {'dp'}, dimensions={0} | all-to-all | bytes 3145728 | tf_op jit(solution)/shard_map/cond/branch_1_fun/all_to_all | solution.py:349
  78.7 1.9 %docs.4 = (f32[128,1024]{1,0:T(8,128)S(1)}, bf16[128,1024]{1,0:T(8,128)(2,1)S(1)}, f32[16,128]{1,0:T(8,128)S(1)}) custom-call(s32[6]{0:T(128)S(1)} %get-tuple-element.114.info_ref, bf16[128,1024]{1,0:T(8,128)(2,1)S(1)} %get-tuple-element.115.other_any, bf16[16,1024]{1,0:T(8,128)(2,1)S(1)} %get-tuple-element.116.pick_ref, ...), custom_call_target="tpu_custom_call" | custom-call | tf_op jit(solution)/shard_map/cond/branch_1_fun/docs/pallas_call | solution.py:39
  80.6 1.3 %collective-permute-start.1 = (bf16[128,1024]{1,0:T(8,128)(2,1)S(1)}, bf16[128,1024]{1,0:T(8,128)(2,1)S(1)}, u32[]{:S(2)}, u32[]{:S(2)}) collective-permute-start(bf16[128,1024]{1,0:T(8,128)(2,1)S(1)} %get-tuple-element.133), channel_id=1, source_target_pairs={{0,1},{1,0},{2,3},{3,2},{4,5},{5,4},{6,7},{7,6},{8,9},{9,8},{10,11... | collective-permute-start | bytes 786440 | tf_op jit(solution)/shard_map/cond/branch_1_fun/ppermute | solution.py:488
  82.0 1.3 %queries.4 = f32[128,1024]{1,0:T(8,128)} custom-call(f32[16,128]{1,0:T(8,128)S(1)} %get-tuple-element.125.sums_ref, bf16[128,1024]{1,0:T(8,128)(2,1)S(1)} %get-tuple-element.126.q_ref, f32[128,2]{1,0:T(8,128)S(1)} %get-tuple-element.127.inv_ref, f32[128,128]{1,0:T(8,128)S(1)} %get-tuple-element.121.e_own_ref, f32[2,128,128]{2,1,0:T(8,128)S(1)} %get-tuple-element.128.e_ref, ...), custom_call_target="tpu_custom_call" | custom-call | tf_op jit(solution)/shard_map/cond/branch_1_fun/queries/pallas_call | solution.py:39
  83.3 1.0 %final.5 = f32[128,1024]{1,0:T(8,128)} custom-call(bf16[128,1024]{1,0:T(8,128)(2,1)S(1)} %get-tuple-element.131.d_ref, f32[128,2]{1,0:T(8,128)S(1)} %get-tuple-element.127.inv_ref, f32[128,1024]{1,0:T(8,128)S(1)} %get-tuple-element.132.acc_ref, bf16[128,1024]{1,0:T(8,128)(2,1)S(1)} %collective-permute-done.1.swapped_ref), custom_call_target="tpu_custom_call" | custom-call | tf_op jit(solution)/shard_map/cond/branch_1_fun/final/pallas_call | solution.py:39
  (30 shorter events, 1.2 us)
Async XLA Ops:
  0.6 22.3 %copy-start = (bf16[128,1024]{1,0:T(8,128)(2,1)S(1)}, bf16[128,1024]{1,0:T(8,128)(2,1)}, u32[]{:S(2)}) copy-start(bf16[128,1024]{1,0:T(8,128)(2,1)} %d_ref.1) | copy-start | bytes 786436
  0.6 22.3 %copy-start.1 = (bf16[128,1024]{1,0:T(8,128)(2,1)S(1)}, bf16[128,1024]{1,0:T(8,128)(2,1)}, u32[]{:S(2)}) copy-start(bf16[128,1024]{1,0:T(8,128)(2,1)} %q_ref.1) | copy-start | bytes 786436
  0.6 22.3 %all-to-all-start.9 = ((bf16[128,8,128]{2,1,0:T(8,128)(2,1)}), bf16[128,8,128]{2,1,0:T(8,128)(2,1)S(1)}, u32[]{:S(2)}, u32[]{:S(2)}) async-start(bf16[128,8,128]{2,1,0:T(8,128)(2,1)} %bitcast.41), calls=%async_computation.9 | async-start | bytes 524288 | tf_op jit(solution)/shard_map/all_to_all | solution.py:349
  13.6 9.3 %collective-permute-start.3 = (bf16[128,1024]{1,0:T(8,128)(2,1)S(1)}, bf16[128,1024]{1,0:T(8,128)(2,1)S(1)}, u32[]{:S(2)}, u32[]{:S(2)}) collective-permute-start(bf16[128,1024]{1,0:T(8,128)(2,1)S(1)} %get-tuple-element.195), channel_id=1, source_target_pairs={{0,1},{1,0},{2,3},{3,2},{4,5},{5,4},{6,7},{7,6},{8,9},{9,8},{10,11... | collective-permute-start | bytes 786440 | tf_op jit(solution)/shard_map/ppermute | solution.py:488
  80.6 2.6 %collective-permute-start.1 = (bf16[128,1024]{1,0:T(8,128)(2,1)S(1)}, bf16[128,1024]{1,0:T(8,128)(2,1)S(1)}, u32[]{:S(2)}, u32[]{:S(2)}) collective-permute-start(bf16[128,1024]{1,0:T(8,128)(2,1)S(1)} %get-tuple-element.133), channel_id=1, source_target_pairs={{0,1},{1,0},{2,3},{3,2},{4,5},{5,4},{6,7},{7,6},{8,9},{9,8},{10,11... | collective-permute-start | bytes 786440 | tf_op jit(solution)/shard_map/cond/branch_1_fun/ppermute | solution.py:488

commit v5 on v4

--- a/solution.py
+++ b/solution.py
@@ -197,14 +197,19 @@
     gd_ref[...] = unit_grad(d_ref[...].astype(jnp.float32), inv_ref[:, 1:2], doc)
 
 
-def first_gather_kernel(cols_ref, spread_ref, query_ref, out_ref):
+def first_gather_kernel(cols_any, spread_ref, query_ref, out_ref, cols_ref, sem):
+    bring = pltpu.make_async_copy(cols_any, cols_ref, sem)
+    bring.start()
+    out_ref[:, 2 * SUB :, :] = query_ref[...]
+    bring.wait()
+
     def step(dest, carry):
-        tiles = [spread_ref[cols_ref[2 * dest + k]] for k in range(2)] + [query_ref[dest]]
+        tiles = [spread_ref[cols_ref[2 * dest + k]] for k in range(2)]
         for slot, tile in enumerate(tiles):
             out_ref[dest, slot * SUB : (slot + 1) * SUB, :] = tile
         return carry
 
-    lax.fori_loop(0, out_ref.shape[0], step, 0, unroll=8)
+    lax.fori_loop(0, out_ref.shape[0], step, 0, unroll=16)
 
 
 def eye_mask(n):
@@ -230,8 +235,11 @@
 
 
 def row_side_kernel(
-    table_ref, qu_ref, du_ref, e_own_ref, et_own_ref, fetched_ref, send_ref, e_ref, row_ref, units_ref, extra_ref
+    table_any, qu_ref, du_ref, e_own_ref, et_own_ref, fetched_ref,
+    send_ref, e_ref, row_ref, units_ref, extra_ref, table_ref, sem
 ):
+    bring = pltpu.make_async_copy(table_any, table_ref, sem)
+    bring.start()
     rows, features = qu_ref.shape
     row_tiles, col_tiles = rows // SUB, features // LANES
     shared = send_ref.shape[1] // SUB - 1
@@ -242,7 +250,8 @@
     row_total = jnp.sum(e_own_ref[...], axis=1, keepdims=True)
     columns = [to_lanes(jnp.sum(et_own_ref[...], axis=1, keepdims=True), eye)]
     for k in range(2):
-        wide = fetched_rows(fetched_ref, k, row_tiles, col_tiles)
+        piece = fetched_ref[...].reshape(row_tiles, col_tiles, 3, SUB, LANES)[:, :, k : k + 1]
+        wide = from_pieces(piece.astype(jnp.float32), 0)
         unit = (wide * inverse_norm(wide)).astype(jnp.bfloat16)
         units_ref[(k + 1) * rows : (k + 2) * rows] = unit
         e = jnp.exp(LOGIT_SCALE * dot_nt(q, unit))
@@ -257,10 +266,10 @@
     extra_ref[...] = jnp.concatenate(doubled, axis=0).astype(jnp.bfloat16)
     send_ref[:, shared * SUB :, :] = jnp.broadcast_to(extra_ref[...][None], (send_ref.shape[0], SUB, LANES))
 
+    bring.wait()
+
     def step(dest, carry):
-        tiles = [
-            fetched_ref[table_ref[dest * stride + slot], 2 * SUB : 3 * SUB, :] for slot in range(shared)
-        ]
+        tiles = [fetched_ref[table_ref[dest * stride + slot]] for slot in range(shared)]
         for slot, tile in enumerate(tiles):
             send_ref[dest, slot * SUB : (slot + 1) * SUB, :] = tile
         return carry
@@ -269,11 +278,13 @@
 
 
 def doc_side_kernel(
-    info_ref, other_any, pick_ref, qu_ref, du_ref, et_own_ref, recv_ref,
-    acc_ref, partner_ref, sums_ref, units_ref, other_ref, sem
+    info_any, other_any, pick_ref, qu_ref, du_ref, et_own_ref, recv_ref,
+    acc_ref, partner_ref, sums_ref, units_ref, other_ref, sem, info_ref, info_sem
 ):
     bring = pltpu.make_async_copy(other_any, other_ref, sem)
     bring.start()
+    bring_info = pltpu.make_async_copy(info_any, info_ref, info_sem)
+    bring_info.start()
     rows, features = qu_ref.shape
     row_tiles, col_tiles = rows // SUB, features // LANES
     blocks = recv_ref.shape[0]
@@ -292,6 +303,7 @@
     units_ref[0:rows] = q
     weights = [[own.astype(jnp.bfloat16)], [jnp.zeros((rows, rows), jnp.bfloat16)]]
     bring.wait()
+    bring_info.wait()
     for slot in range(shared):
         entry = info_ref[slot]
         side = 1 - lax.rem(entry, 2)
@@ -396,10 +408,20 @@
     return tiled.reshape(-1, SUB, LANES)
 
 
+def small_table(x):
+    return pltpu.SMEM(x.shape, x.dtype), pltpu.SemaphoreType.DMA
+
+
 def fetch(cols, spread, query_unit):
     blocks = lax.axis_size("dp")
     wanted = vmem_call(
-        first_gather_kernel, pltpu.VMEM((blocks, 3 * SUB, LANES), jnp.bfloat16), 1, 2, name="gather"
+        first_gather_kernel,
+        pltpu.VMEM((blocks, 3 * SUB, LANES), jnp.bfloat16),
+        0,
+        2,
+        small_table(cols),
+        name="gather",
+        n_any=1,
     )(cols, spread, pieces(query_unit))
     return exchange(wanted)
 
@@ -454,24 +476,26 @@
             sds((rows, 1), f32),
             sds((3 * rows, features), bf16),
         ),
-        1,
+        0,
         5,
-        (pltpu.VMEM((SUB, LANES), bf16),),
+        (pltpu.VMEM((SUB, LANES), bf16), *small_table(table)),
         name="rows",
-    )(table, qu, du, e_own, et_own, fetched)
+        n_any=1,
+    )(table, qu, du, e_own, et_own, fetched.reshape(3 * blocks, SUB, LANES))
     recv = exchange(send)
     acc, partner, sums = vmem_call(
         doc_side_kernel,
         (sds((rows, features), f32), wide, sds((PICKS, LANES), f32)),
-        1,
+        0,
         5,
         (
             pltpu.VMEM(((shared + 1) * rows, features), bf16),
             pltpu.VMEM((rows, features), bf16),
             pltpu.SemaphoreType.DMA,
+            *small_table(info),
         ),
         name="docs",
-        n_any=1,
+        n_any=2,
     )(info, other, picks, qu, du, et_own, recv)
     swapped = swap_cores(partner)
     grad_scratch = (pltpu.VMEM((rows, features), f32), pltpu.SemaphoreType.DMA((4,)))
@@ -505,7 +529,8 @@
     table, deepest = shared_slots(cols, blocks)
     info = lax.dynamic_index_in_dim(table, me, 0, keepdims=False)
     picks = message_picks(cols, info, me, blocks)
-    table = (jnp.maximum(table - 1, 0) // 2).reshape(-1)
+    table = jnp.pad(3 * (jnp.maximum(table - 1, 0) // 2) + 2, ((0, 0), (0, SUB - SHARED))).reshape(-1)
+    info = jnp.pad(info, (0, LANES - SHARED))
     choice = sum((deepest >= 2 * shared).astype(jnp.int32) for shared in CHOICES)
     spread, cols, table, info, picks, choice, own = lax.optimization_barrier(
         (spread, cols, table, info, picks, choice, own)

time: 85.1 us -> 84.5 us (level)
  Pallas kernels: 8.72 us -> 7.81 us
    pallas_call x5, Pallas kernels: 7.23 us -> 6.33 us  [run(): return call(*args[:n_smem + n_any], *kept)]
  transfers between devices with their start and end apart: 3 -> 3, of which waited for: 1 -> 1; matrix products, arithmetic and copies ran while one was open for 5% -> 6% of each run, Pallas kernels for 3% -> 3%
where the time goes in v5:
time: 84.5 us; the launch traced here: 84.2 us
  blocking collectives  53.1 us (63%)
  starting transfers between devices  14 us (17%)
  Pallas kernels  7.81 us (9%)
  between operations  2.94 us (3%)
  local copies, waits for them, and re-layouts  2.54 us (3%)
  other arithmetic  2.37 us (3%)
  waiting for transfers between devices  1.2 us (1%)
    all_to_all x2, blocking collectives, exchange(): return lax.all_to_all(x, 'dp', split_axis=0, concat_axis=0, tiled=True)  53.1 us
    all_to_all x1, starting transfers between devices, exchange(): return lax.all_to_all(x, 'dp', split_axis=0, concat_axis=0, tiled=True)  11.5 us
    pallas_call x5, Pallas kernels, run(): return call(*args[:n_smem + n_any], *kept)  6.33 us
    ppermute x2, starting transfers between devices, swap_cores(): lax.ppermute(x, 'dp', [(i, i ^ 1) for i in range(lax.axis_size('dp'))])  2.46 us
  transfers between devices with their start and end apart: 3, of which 1 were waited for; matrix products, arithmetic and copies ran while one was open for 6% of the time, Pallas kernels for 3%

profile of v5, /device:TPU:1, one launch (start us, length us, event | category | flops | bytes accessed | tf_op | source)
XLA Modules:
  0.0 84.2 jit_solution(9031026727835461844)
XLA Ops:
  0.6 11.5 %all-to-all-start.9 = ((bf16[128,8,128]{2,1,0:T(8,128)(2,1)}), bf16[128,8,128]{2,1,0:T(8,128)(2,1)S(1)}, u32[]{:S(2)}, u32[]{:S(2)}) async-start(bf16[128,8,128]{2,1,0:T(8,128)(2,1)} %bitcast.44), calls=%async_computation.9 | async-start | bytes 524288 | tf_op jit(solution)/shard_map/all_to_all | solution.py:361
  12.1 1.5 %own.1 = (bf16[128,1024]{1,0:T(8,128)(2,1)S(1)}, bf16[128,1024]{1,0:T(8,128)(2,1)S(1)}, f32[128,2]{1,0:T(8,128)S(1)}, f32[128,128]{1,0:T(8,128)S(1)}, f32[128,128]{1,0:T(8,128)S(1)}) custom-call(bf16[128,1024]{1,0:T(8,128)(2,1)} %q_ref.1, bf16[128,1024]{1,0:T(8,128)(2,1)} %d_ref.1), custom_call_target="tpu_custom_call" | custom-call | tf_op jit(solution)/shard_map/own/pallas_call | solution.py:37
  13.6 1.1 %collective-permute-start.3 = (bf16[128,1024]{1,0:T(8,128)(2,1)S(1)}, bf16[128,1024]{1,0:T(8,128)(2,1)S(1)}, u32[]{:S(2)}, u32[]{:S(2)}) collective-permute-start(bf16[128,1024]{1,0:T(8,128)(2,1)S(1)} %get-tuple-element.195), channel_id=1, source_target_pairs={{0,1},{1,0},{2,3},{3,2},{4,5},{5,4},{6,7},{7,6},{8,9},{9,8},{10,11... | collective-permute-start | bytes 786440 | tf_op jit(solution)/shard_map/ppermute | solution.py:512
  14.8 0.8 fusion.17
  15.6 0.7 iota_compare_fusion.3
  16.3 0.1 lt.75
  16.9 0.1 select_reduce_fusion.2
  17.2 0.2 dynamic-slice_reduce_fusion
  17.4 0.1 reshape.287
  17.5 0.2 convert_reduce_fusion
  17.7 0.6 fusion.18
  18.4 0.2 select_reduce_fusion
  18.6 0.1 reshape.288
  18.9 0.1 reshape.290
  21.8 1.2 %all-to-all-done.9 = bf16[128,8,128]{2,1,0:T(8,128)(2,1)S(1)} async-done(((bf16[128,8,128]{2,1,0:T(8,128)(2,1)}), bf16[128,8,128]{2,1,0:T(8,128)(2,1)S(1)}, u32[]{:S(2)}, u32[]{:S(2)}) %all-to-all-start.9) | async-done | bytes 262176 | tf_op jit(solution)/shard_map/all_to_all | solution.py:361
  23.0 61.1 %conditional.1 = ((f32[128,1024]{1,0:T(8,128)}, f32[128,1024]{1,0:T(8,128)})) conditional(s32[]{:T(128)} %clamp.3, (bf16[128,1024]{1,0:T(8,128)(2,1)S(1)}, s32[256]{0:T(256)S(1)}, bf16[128,8,128]{2,1,0:T(8,128)(2,1)S(1)}, s32[1024]{0:T(1024)S(1)}, bf16[128,1024]{1,0:T(8,128)(2,1)S(1)}, ...), branch_computations={%region_5.6_spmd, %region_6.7_spmd, %region_7.8_spmd, %region_8.9_... | conditional | bytes 6291520 | solution.py:540
  23.0 0.9 %gather.5 = bf16[128,24,128]{2,1,0:T(8,128)(2,1)S(1)} custom-call(s32[256]{0:T(256)S(1)} %get-tuple-element.122.cols_any, bf16[128,8,128]{2,1,0:T(8,128)(2,1)S(1)} %get-tuple-element.123.spread_ref, bf16[128,8,128]{2,1,0:T(8,128)(2,1)S(1)} %bitcast.41), custom_call_target="tpu_custom_call" | custom-call | tf_op jit(solution)/shard_map/cond/branch_1_fun/gather/pallas_call | solution.py:39
  23.9 23.8 %all_to_all.43 = bf16[128,24,128]{2,1,0:T(8,128)(2,1)S(1)} all-to-all(bf16[128,24,128]{2,1,0:T(8,128)(2,1)S(1)} %gather.5), channel_id=1, replica_groups=mesh['dp'=128] {'dp'}, dimensions={0} | all-to-all | bytes 1572864 | tf_op jit(solution)/shard_map/cond/branch_1_fun/all_to_all | solution.py:361
  47.7 1.5 %rows.4 = (bf16[128,48,128]{2,1,0:T(8,128)(2,1)S(1)}, f32[2,128,128]{2,1,0:T(8,128)S(1)}, f32[128,1]{1,0:T(8,128)S(1)}, bf16[384,1024]{1,0:T(8,128)(2,1)S(1)}) custom-call(s32[1024]{0:T(1024)S(1)} %get-tuple-element.120.table_any, bf16[128,1024]{1,0:T(8,128)(2,1)S(1)} %get-tuple-element.117.qu_ref, bf16[128,1024]{1,0:T(8,128)(2,1)S(1)} %get-tuple-element.118.du_ref, ...), custom_call_target="tpu_custom_call" | custom-call | tf_op jit(solution)/shard_map/cond/branch_1_fun/rows/pallas_call | solution.py:39
  49.2 29.2 %all_to_all.44.recv_ref = bf16[128,48,128]{2,1,0:T(8,128)(2,1)S(1)} all-to-all(bf16[128,48,128]{2,1,0:T(8,128)(2,1)S(1)} %get-tuple-element.124), channel_id=1, replica_groups=mesh['dp'=128] {'dp'}, dimensions={0} | all-to-all | bytes 3145728 | tf_op jit(solution)/shard_map/cond/branch_1_fun/all_to_all | solution.py:361
  78.4 1.7 %docs.4 = (f32[128,1024]{1,0:T(8,128)S(1)}, bf16[128,1024]{1,0:T(8,128)(2,1)S(1)}, f32[16,128]{1,0:T(8,128)S(1)}) custom-call(s32[128]{0:T(128)S(1)} %get-tuple-element.114.info_any, bf16[128,1024]{1,0:T(8,128)(2,1)S(1)} %get-tuple-element.115.other_any, bf16[16,1024]{1,0:T(8,128)(2,1)S(1)} %get-tuple-element.116.pick_ref, ...), custom_call_target="tpu_custom_call" | custom-call | tf_op jit(solution)/shard_map/cond/branch_1_fun/docs/pallas_call | solution.py:39
  80.1 1.3 %collective-permute-start.1 = (bf16[128,1024]{1,0:T(8,128)(2,1)S(1)}, bf16[128,1024]{1,0:T(8,128)(2,1)S(1)}, u32[]{:S(2)}, u32[]{:S(2)}) collective-permute-start(bf16[128,1024]{1,0:T(8,128)(2,1)S(1)} %get-tuple-element.133), channel_id=1, source_target_pairs={{0,1},{1,0},{2,3},{3,2},{4,5},{5,4},{6,7},{7,6},{8,9},{9,8},{10,11... | collective-permute-start | bytes 786440 | tf_op jit(solution)/shard_map/cond/branch_1_fun/ppermute | solution.py:512
  81.4 1.3 %queries.4 = f32[128,1024]{1,0:T(8,128)} custom-call(f32[16,128]{1,0:T(8,128)S(1)} %get-tuple-element.125.sums_ref, bf16[128,1024]{1,0:T(8,128)(2,1)S(1)} %get-tuple-element.126.q_ref, f32[128,2]{1,0:T(8,128)S(1)} %get-tuple-element.127.inv_ref, f32[128,128]{1,0:T(8,128)S(1)} %get-tuple-element.121.e_own_ref, f32[2,128,128]{2,1,0:T(8,128)S(1)} %get-tuple-element.128.e_ref, ...), custom_call_target="tpu_custom_call" | custom-call | tf_op jit(solution)/shard_map/cond/branch_1_fun/queries/pallas_call | solution.py:39
  82.7 1.0 %final.5 = f32[128,1024]{1,0:T(8,128)} custom-call(bf16[128,1024]{1,0:T(8,128)(2,1)S(1)} %get-tuple-element.131.d_ref, f32[128,2]{1,0:T(8,128)S(1)} %get-tuple-element.127.inv_ref, f32[128,1024]{1,0:T(8,128)S(1)} %get-tuple-element.132.acc_ref, bf16[128,1024]{1,0:T(8,128)(2,1)S(1)} %collective-permute-done.1.swapped_ref), custom_call_target="tpu_custom_call" | custom-call | tf_op jit(solution)/shard_map/cond/branch_1_fun/final/pallas_call | solution.py:39
  (35 shorter events, 1.5 us)
Async XLA Ops:
  0.6 22.3 %copy-start = (bf16[128,1024]{1,0:T(8,128)(2,1)S(1)}, bf16[128,1024]{1,0:T(8,128)(2,1)}, u32[]{:S(2)}) copy-start(bf16[128,1024]{1,0:T(8,128)(2,1)} %d_ref.1) | copy-start | bytes 786436
  0.6 22.3 %copy-start.1 = (bf16[128,1024]{1,0:T(8,128)(2,1)S(1)}, bf16[128,1024]{1,0:T(8,128)(2,1)}, u32[]{:S(2)}) copy-start(bf16[128,1024]{1,0:T(8,128)(2,1)} %q_ref.1) | copy-start | bytes 786436
  0.6 22.3 %all-to-all-start.9 = ((bf16[128,8,128]{2,1,0:T(8,128)(2,1)}), bf16[128,8,128]{2,1,0:T(8,128)(2,1)S(1)}, u32[]{:S(2)}, u32[]{:S(2)}) async-start(bf16[128,8,128]{2,1,0:T(8,128)(2,1)} %bitcast.44), calls=%async_computation.9 | async-start | bytes 524288 | tf_op jit(solution)/shard_map/all_to_all | solution.py:361
  13.6 9.3 %collective-permute-start.3 = (bf16[128,1024]{1,0:T(8,128)(2,1)S(1)}, bf16[128,1024]{1,0:T(8,128)(2,1)S(1)}, u32[]{:S(2)}, u32[]{:S(2)}) collective-permute-start(bf16[128,1024]{1,0:T(8,128)(2,1)S(1)} %get-tuple-element.195), channel_id=1, source_target_pairs={{0,1},{1,0},{2,3},{3,2},{4,5},{5,4},{6,7},{7,6},{8,9},{9,8},{10,11... | collective-permute-start | bytes 786440 | tf_op jit(solution)/shard_map/ppermute | solution.py:512
  80.1 2.6 %collective-permute-start.1 = (bf16[128,1024]{1,0:T(8,128)(2,1)S(1)}, bf16[128,1024]{1,0:T(8,128)(2,1)S(1)}, u32[]{:S(2)}, u32[]{:S(2)}) collective-permute-start(bf16[128,1024]{1,0:T(8,128)(2,1)S(1)} %get-tuple-element.133), channel_id=1, source_target_pairs={{0,1},{1,0},{2,3},{3,2},{4,5},{5,4},{6,7},{7,6},{8,9},{9,8},{10,11... | collective-permute-start | bytes 786440 | tf_op jit(solution)/shard_map/cond/branch_1_fun/ppermute | solution.py:512

commit v6 on v5

--- a/solution.py
+++ b/solution.py
@@ -383,7 +383,8 @@
     place = device * SHARED + slot
     hit = (place[None, :] == jnp.arange(blocks * SHARED)[:, None]) & (slot[None, :] < SHARED)
     table = jnp.sum(jnp.where(hit, entry[None, :], 0), axis=1).astype(jnp.int32)
-    return table.reshape(blocks, SHARED), jnp.max(rank)
+    level = sum((rank >= 2 * shared).astype(jnp.int32) for shared in CHOICES)
+    return table.reshape(blocks, SHARED), jnp.max(level)
 
 
 def message_picks(cols, mine, me, blocks):
@@ -526,12 +527,11 @@
         own_pair_kernel, (wide, wide, pltpu.VMEM((rows, 2), jnp.float32), mat, mat), 0, 2, name="own", keep=False
     )(query_emb, doc_emb)
     own = (*own, swap_cores(own[1]))
-    table, deepest = shared_slots(cols, blocks)
+    table, choice = shared_slots(cols, blocks)
     info = lax.dynamic_index_in_dim(table, me, 0, keepdims=False)
     picks = message_picks(cols, info, me, blocks)
     table = jnp.pad(3 * (jnp.maximum(table - 1, 0) // 2) + 2, ((0, 0), (0, SUB - SHARED))).reshape(-1)
     info = jnp.pad(info, (0, LANES - SHARED))
-    choice = sum((deepest >= 2 * shared).astype(jnp.int32) for shared in CHOICES)
     spread, cols, table, info, picks, choice, own = lax.optimization_barrier(
         (spread, cols, table, info, picks, choice, own)
     )

time: 84.5 us -> 83.2 us (0.985)
  blocking collectives: 53.1 us -> 51.1 us
  waiting for transfers between devices: 1.2 us -> 3.15 us
  between operations: 2.94 us -> 1.65 us
    all_to_all x2, blocking collectives: 53.1 us -> 51.1 us  [exchange(): return lax.all_to_all(x, 'dp', split_axis=0, concat_axis=0, tiled=True)]
    all_to_all x1, waiting for transfers between devices: 1.19 us -> 3.14 us  [exchange(): return lax.all_to_all(x, 'dp', split_axis=0, concat_axis=0, tiled=True)]
where the time goes in v6:
time: 83.2 us; the launch traced here: 82.9 us
  blocking collectives  51.1 us (61%)
  starting transfers between devices  13.9 us (17%)
  Pallas kernels  7.81 us (9%)
  waiting for transfers between devices  3.15 us (4%)
  local copies, waits for them, and re-layouts  2.54 us (3%)
  other arithmetic  2.37 us (3%)
  between operations  1.65 us (2%)
    all_to_all x2, blocking collectives, exchange(): return lax.all_to_all(x, 'dp', split_axis=0, concat_axis=0, tiled=True)  51.1 us
    all_to_all x1, starting transfers between devices, exchange(): return lax.all_to_all(x, 'dp', split_axis=0, concat_axis=0, tiled=True)  11.5 us
    pallas_call x5, Pallas kernels, run(): return call(*args[:n_smem + n_any], *kept)  6.32 us
    all_to_all x1, waiting for transfers between devices, exchange(): return lax.all_to_all(x, 'dp', split_axis=0, concat_axis=0, tiled=True)  3.14 us
    ppermute x2, starting transfers between devices, swap_cores(): lax.ppermute(x, 'dp', [(i, i ^ 1) for i in range(lax.axis_size('dp'))])  2.46 us
  transfers between devices with their start and end apart: 3, of which 1 were waited for; matrix products, arithmetic and copies ran while one was open for 6% of the time, Pallas kernels for 3%

profile of v6, /device:TPU:1, one launch (start us, length us, event | category | flops | bytes accessed | tf_op | source)
XLA Modules:
  0.0 82.9 jit_solution(2098230005911239203)
XLA Ops:
  0.6 11.5 %all-to-all-start.9 = ((bf16[128,8,128]{2,1,0:T(8,128)(2,1)}), bf16[128,8,128]{2,1,0:T(8,128)(2,1)S(1)}, u32[]{:S(2)}, u32[]{:S(2)}) async-start(bf16[128,8,128]{2,1,0:T(8,128)(2,1)} %bitcast.44), calls=%async_computation.9 | async-start | bytes 524288 | tf_op jit(solution)/shard_map/all_to_all | solution.py:361
  12.1 1.5 %own.1 = (bf16[128,1024]{1,0:T(8,128)(2,1)S(1)}, bf16[128,1024]{1,0:T(8,128)(2,1)S(1)}, f32[128,2]{1,0:T(8,128)S(1)}, f32[128,128]{1,0:T(8,128)S(1)}, f32[128,128]{1,0:T(8,128)S(1)}) custom-call(bf16[128,1024]{1,0:T(8,128)(2,1)} %q_ref.1, bf16[128,1024]{1,0:T(8,128)(2,1)} %d_ref.1), custom_call_target="tpu_custom_call" | custom-call | tf_op jit(solution)/shard_map/own/pallas_call | solution.py:37
  13.6 1.1 %collective-permute-start.3 = (bf16[128,1024]{1,0:T(8,128)(2,1)S(1)}, bf16[128,1024]{1,0:T(8,128)(2,1)S(1)}, u32[]{:S(2)}, u32[]{:S(2)}) collective-permute-start(bf16[128,1024]{1,0:T(8,128)(2,1)S(1)} %get-tuple-element.195), channel_id=1, source_target_pairs={{0,1},{1,0},{2,3},{3,2},{4,5},{5,4},{6,7},{7,6},{8,9},{9,8},{10,11... | collective-permute-start | bytes 786440 | tf_op jit(solution)/shard_map/ppermute | solution.py:513
  14.8 0.8 fusion.20
  15.6 0.7 iota_compare_fusion.3
  16.3 0.1 lt.75
  16.9 0.1 select_reduce_fusion.2
  17.2 0.2 dynamic-slice_reduce_fusion
  17.4 0.1 reshape.287
  17.5 0.2 convert_reduce_fusion
  17.7 0.6 fusion.16
  18.4 0.2 select_reduce_fusion
  18.6 0.1 reshape.288
  18.9 0.1 reshape.290
  19.8 3.1 %all-to-all-done.9 = bf16[128,8,128]{2,1,0:T(8,128)(2,1)S(1)} async-done(((bf16[128,8,128]{2,1,0:T(8,128)(2,1)}), bf16[128,8,128]{2,1,0:T(8,128)(2,1)S(1)}, u32[]{:S(2)}, u32[]{:S(2)}) %all-to-all-start.9) | async-done | bytes 262176 | tf_op jit(solution)/shard_map/all_to_all | solution.py:361
  23.6 59.1 %conditional.1 = ((f32[128,1024]{1,0:T(8,128)}, f32[128,1024]{1,0:T(8,128)})) conditional(s32[]{:T(128)} %clamp.3, (bf16[128,1024]{1,0:T(8,128)(2,1)S(1)}, s32[256]{0:T(256)S(1)}, bf16[128,8,128]{2,1,0:T(8,128)(2,1)S(1)}, s32[1024]{0:T(1024)S(1)}, bf16[128,1024]{1,0:T(8,128)(2,1)S(1)}, ...), branch_computations={%region_5.6_spmd, %region_6.7_spmd, %region_7.8_spmd, %region_8.9_... | conditional | bytes 6291520 | solution.py:540
  23.7 0.9 %gather.5 = bf16[128,24,128]{2,1,0:T(8,128)(2,1)S(1)} custom-call(s32[256]{0:T(256)S(1)} %get-tuple-element.122.cols_any, bf16[128,8,128]{2,1,0:T(8,128)(2,1)S(1)} %get-tuple-element.123.spread_ref, bf16[128,8,128]{2,1,0:T(8,128)(2,1)S(1)} %bitcast.41), custom_call_target="tpu_custom_call" | custom-call | tf_op jit(solution)/shard_map/cond/branch_1_fun/gather/pallas_call | solution.py:39
  24.5 21.9 %all_to_all.43 = bf16[128,24,128]{2,1,0:T(8,128)(2,1)S(1)} all-to-all(bf16[128,24,128]{2,1,0:T(8,128)(2,1)S(1)} %gather.5), channel_id=1, replica_groups=mesh['dp'=128] {'dp'}, dimensions={0} | all-to-all | bytes 1572864 | tf_op jit(solution)/shard_map/cond/branch_1_fun/all_to_all | solution.py:361
  46.4 1.5 %rows.4 = (bf16[128,48,128]{2,1,0:T(8,128)(2,1)S(1)}, f32[2,128,128]{2,1,0:T(8,128)S(1)}, f32[128,1]{1,0:T(8,128)S(1)}, bf16[384,1024]{1,0:T(8,128)(2,1)S(1)}) custom-call(s32[1024]{0:T(1024)S(1)} %get-tuple-element.120.table_any, bf16[128,1024]{1,0:T(8,128)(2,1)S(1)} %get-tuple-element.117.qu_ref, bf16[128,1024]{1,0:T(8,128)(2,1)S(1)} %get-tuple-element.118.du_ref, ...), custom_call_target="tpu_custom_call" | custom-call | tf_op jit(solution)/shard_map/cond/branch_1_fun/rows/pallas_call | solution.py:39
  47.9 29.2 %all_to_all.44.recv_ref = bf16[128,48,128]{2,1,0:T(8,128)(2,1)S(1)} all-to-all(bf16[128,48,128]{2,1,0:T(8,128)(2,1)S(1)} %get-tuple-element.124), channel_id=1, replica_groups=mesh['dp'=128] {'dp'}, dimensions={0} | all-to-all | bytes 3145728 | tf_op jit(solution)/shard_map/cond/branch_1_fun/all_to_all | solution.py:361
  77.1 1.7 %docs.4 = (f32[128,1024]{1,0:T(8,128)S(1)}, bf16[128,1024]{1,0:T(8,128)(2,1)S(1)}, f32[16,128]{1,0:T(8,128)S(1)}) custom-call(s32[128]{0:T(128)S(1)} %get-tuple-element.114.info_any, bf16[128,1024]{1,0:T(8,128)(2,1)S(1)} %get-tuple-element.115.other_any, bf16[16,1024]{1,0:T(8,128)(2,1)S(1)} %get-tuple-element.116.pick_ref, ...), custom_call_target="tpu_custom_call" | custom-call | tf_op jit(solution)/shard_map/cond/branch_1_fun/docs/pallas_call | solution.py:39
  78.8 1.3 %collective-permute-start.1 = (bf16[128,1024]{1,0:T(8,128)(2,1)S(1)}, bf16[128,1024]{1,0:T(8,128)(2,1)S(1)}, u32[]{:S(2)}, u32[]{:S(2)}) collective-permute-start(bf16[128,1024]{1,0:T(8,128)(2,1)S(1)} %get-tuple-element.133), channel_id=1, source_target_pairs={{0,1},{1,0},{2,3},{3,2},{4,5},{5,4},{6,7},{7,6},{8,9},{9,8},{10,11... | collective-permute-start | bytes 786440 | tf_op jit(solution)/shard_map/cond/branch_1_fun/ppermute | solution.py:513
  80.1 1.3 %queries.4 = f32[128,1024]{1,0:T(8,128)} custom-call(f32[16,128]{1,0:T(8,128)S(1)} %get-tuple-element.125.sums_ref, bf16[128,1024]{1,0:T(8,128)(2,1)S(1)} %get-tuple-element.126.q_ref, f32[128,2]{1,0:T(8,128)S(1)} %get-tuple-element.127.inv_ref, f32[128,128]{1,0:T(8,128)S(1)} %get-tuple-element.121.e_own_ref, f32[2,128,128]{2,1,0:T(8,128)S(1)} %get-tuple-element.128.e_ref, ...), custom_call_target="tpu_custom_call" | custom-call | tf_op jit(solution)/shard_map/cond/branch_1_fun/queries/pallas_call | solution.py:39
  81.4 1.0 %final.5 = f32[128,1024]{1,0:T(8,128)} custom-call(bf16[128,1024]{1,0:T(8,128)(2,1)S(1)} %get-tuple-element.131.d_ref, f32[128,2]{1,0:T(8,128)S(1)} %get-tuple-element.127.inv_ref, f32[128,1024]{1,0:T(8,128)S(1)} %get-tuple-element.132.acc_ref, bf16[128,1024]{1,0:T(8,128)(2,1)S(1)} %collective-permute-done.1.swapped_ref), custom_call_target="tpu_custom_call" | custom-call | tf_op jit(solution)/shard_map/cond/branch_1_fun/final/pallas_call | solution.py:39
  (35 shorter events, 1.5 us)
Async XLA Ops:
  0.6 23.0 %copy-start = (bf16[128,1024]{1,0:T(8,128)(2,1)S(1)}, bf16[128,1024]{1,0:T(8,128)(2,1)}, u32[]{:S(2)}) copy-start(bf16[128,1024]{1,0:T(8,128)(2,1)} %d_ref.1) | copy-start | bytes 786436
  0.6 23.0 %copy-start.1 = (bf16[128,1024]{1,0:T(8,128)(2,1)S(1)}, bf16[128,1024]{1,0:T(8,128)(2,1)}, u32[]{:S(2)}) copy-start(bf16[128,1024]{1,0:T(8,128)(2,1)} %q_ref.1) | copy-start | bytes 786436
  0.6 22.3 %all-to-all-start.9 = ((bf16[128,8,128]{2,1,0:T(8,128)(2,1)}), bf16[128,8,128]{2,1,0:T(8,128)(2,1)S(1)}, u32[]{:S(2)}, u32[]{:S(2)}) async-start(bf16[128,8,128]{2,1,0:T(8,128)(2,1)} %bitcast.44), calls=%async_computation.9 | async-start | bytes 524288 | tf_op jit(solution)/shard_map/all_to_all | solution.py:361
  13.6 9.3 %collective-permute-start.3 = (bf16[128,1024]{1,0:T(8,128)(2,1)S(1)}, bf16[128,1024]{1,0:T(8,128)(2,1)S(1)}, u32[]{:S(2)}, u32[]{:S(2)}) collective-permute-start(bf16[128,1024]{1,0:T(8,128)(2,1)S(1)} %get-tuple-element.195), channel_id=1, source_target_pairs={{0,1},{1,0},{2,3},{3,2},{4,5},{5,4},{6,7},{7,6},{8,9},{9,8},{10,11... | collective-permute-start | bytes 786440 | tf_op jit(solution)/shard_map/ppermute | solution.py:513
  78.8 2.6 %collective-permute-start.1 = (bf16[128,1024]{1,0:T(8,128)(2,1)S(1)}, bf16[128,1024]{1,0:T(8,128)(2,1)S(1)}, u32[]{:S(2)}, u32[]{:S(2)}) collective-permute-start(bf16[128,1024]{1,0:T(8,128)(2,1)S(1)} %get-tuple-element.133), channel_id=1, source_target_pairs={{0,1},{1,0},{2,3},{3,2},{4,5},{5,4},{6,7},{7,6},{8,9},{9,8},{10,11... | collective-permute-start | bytes 786440 | tf_op jit(solution)/shard_map/cond/branch_1_fun/ppermute | solution.py:513

commit v7 on v6

--- a/solution.py
+++ b/solution.py
@@ -279,9 +279,9 @@
 
 def doc_side_kernel(
     info_any, other_any, pick_ref, qu_ref, du_ref, et_own_ref, recv_ref,
-    acc_ref, partner_ref, sums_ref, units_ref, other_ref, sem, info_ref, info_sem
+    acc_ref, partner_ref, sums_ref, units_ref, pair_ref, sem, info_ref, info_sem
 ):
-    bring = pltpu.make_async_copy(other_any, other_ref, sem)
+    bring = pltpu.make_async_copy(other_any, pair_ref.at[1], sem)
     bring.start()
     bring_info = pltpu.make_async_copy(info_any, info_ref, info_sem)
     bring_info.start()
@@ -301,6 +301,7 @@
     q = qu_ref[...]
     own = weight(et_own_ref[...], sums[4:5], inverse[0]) - jnp.where(eye, 1.0, 0.0)
     units_ref[0:rows] = q
+    pair_ref[0] = du_ref[...]
     weights = [[own.astype(jnp.bfloat16)], [jnp.zeros((rows, rows), jnp.bfloat16)]]
     bring.wait()
     bring_info.wait()
@@ -309,7 +310,7 @@
         side = 1 - lax.rem(entry, 2)
         unit = fetched_rows(recv_ref, slot, row_tiles, col_tiles).astype(jnp.bfloat16)
         units_ref[(slot + 1) * rows : (slot + 2) * rows] = unit
-        docs = jnp.where(side == 1, other_ref[...], du_ref[...])
+        docs = pair_ref[side]
         et = jnp.exp(LOGIT_SCALE * dot_nt(docs, unit))
         live = entry > 0
         total = jnp.where(live, sums[5 + slot : 6 + slot], 1.0)
@@ -491,7 +492,7 @@
         5,
         (
             pltpu.VMEM(((shared + 1) * rows, features), bf16),
-            pltpu.VMEM((rows, features), bf16),
+            pltpu.VMEM((2, rows, features), bf16),
             pltpu.SemaphoreType.DMA,
             *small_table(info),
         ),

time: 83.2 us -> 84.8 us (1.019); the launches traced: 82.9 us -> 86.2 us
  blocking collectives: 51.1 us -> 53.9 us
    all_to_all x2, blocking collectives: 51.1 us -> 53.9 us  [exchange(): return lax.all_to_all(x, 'dp', split_axis=0, concat_axis=0, tiled=True)]
where the time goes in v7:
time: 84.8 us; the launch traced here: 86.2 us
  blocking collectives  53.9 us (64%)
  starting transfers between devices  14 us (17%)
  Pallas kernels  8.02 us (9%)
  waiting for transfers between devices  3.15 us (4%)
  local copies, waits for them, and re-layouts  2.54 us (3%)
  other arithmetic  2.37 us (3%)
  between operations  1.65 us (2%)
    all_to_all x2, blocking collectives, exchange(): return lax.all_to_all(x, 'dp', split_axis=0, concat_axis=0, tiled=True)  53.9 us
    all_to_all x1, starting transfers between devices, exchange(): return lax.all_to_all(x, 'dp', split_axis=0, concat_axis=0, tiled=True)  11.5 us
    pallas_call x5, Pallas kernels, run(): return call(*args[:n_smem + n_any], *kept)  6.53 us
    all_to_all x1, waiting for transfers between devices, exchange(): return lax.all_to_all(x, 'dp', split_axis=0, concat_axis=0, tiled=True)  3.14 us
    ppermute x2, starting transfers between devices, swap_cores(): lax.ppermute(x, 'dp', [(i, i ^ 1) for i in range(lax.axis_size('dp'))])  2.46 us
  transfers between devices with their start and end apart: 3, of which 1 were waited for; matrix products, arithmetic and copies ran while one was open for 6% of the time, Pallas kernels for 3%

profile of v7, /device:TPU:1, one launch (start us, length us, event | category | flops | bytes accessed | tf_op | source)
XLA Modules:
  0.0 86.2 jit_solution(6685140973027461404)
XLA Ops:
  0.6 11.5 %all-to-all-start.9 = ((bf16[128,8,128]{2,1,0:T(8,128)(2,1)}), bf16[128,8,128]{2,1,0:T(8,128)(2,1)S(1)}, u32[]{:S(2)}, u32[]{:S(2)}) async-start(bf16[128,8,128]{2,1,0:T(8,128)(2,1)} %bitcast.44), calls=%async_computation.9 | async-start | bytes 524288 | tf_op jit(solution)/shard_map/all_to_all | solution.py:362
  12.1 1.5 %own.1 = (bf16[128,1024]{1,0:T(8,128)(2,1)S(1)}, bf16[128,1024]{1,0:T(8,128)(2,1)S(1)}, f32[128,2]{1,0:T(8,128)S(1)}, f32[128,128]{1,0:T(8,128)S(1)}, f32[128,128]{1,0:T(8,128)S(1)}) custom-call(bf16[128,1024]{1,0:T(8,128)(2,1)} %q_ref.1, bf16[128,1024]{1,0:T(8,128)(2,1)} %d_ref.1), custom_call_target="tpu_custom_call" | custom-call | tf_op jit(solution)/shard_map/own/pallas_call | solution.py:37
  13.6 1.1 %collective-permute-start.3 = (bf16[128,1024]{1,0:T(8,128)(2,1)S(1)}, bf16[128,1024]{1,0:T(8,128)(2,1)S(1)}, u32[]{:S(2)}, u32[]{:S(2)}) collective-permute-start(bf16[128,1024]{1,0:T(8,128)(2,1)S(1)} %get-tuple-element.195), channel_id=1, source_target_pairs={{0,1},{1,0},{2,3},{3,2},{4,5},{5,4},{6,7},{7,6},{8,9},{9,8},{10,11... | collective-permute-start | bytes 786440 | tf_op jit(solution)/shard_map/ppermute | solution.py:514
  14.8 0.8 fusion.20
  15.6 0.7 iota_compare_fusion.3
  16.3 0.1 lt.75
  16.9 0.1 select_reduce_fusion.2
  17.2 0.2 dynamic-slice_reduce_fusion
  17.4 0.1 reshape.287
  17.5 0.2 convert_reduce_fusion
  17.7 0.6 fusion.16
  18.4 0.2 select_reduce_fusion
  18.6 0.1 reshape.288
  18.9 0.1 reshape.290
  19.8 3.1 %all-to-all-done.9 = bf16[128,8,128]{2,1,0:T(8,128)(2,1)S(1)} async-done(((bf16[128,8,128]{2,1,0:T(8,128)(2,1)}), bf16[128,8,128]{2,1,0:T(8,128)(2,1)S(1)}, u32[]{:S(2)}, u32[]{:S(2)}) %all-to-all-start.9) | async-done | bytes 262176 | tf_op jit(solution)/shard_map/all_to_all | solution.py:362
  23.6 62.3 %conditional.1 = ((f32[128,1024]{1,0:T(8,128)}, f32[128,1024]{1,0:T(8,128)})) conditional(s32[]{:T(128)} %clamp.3, (bf16[128,1024]{1,0:T(8,128)(2,1)S(1)}, s32[256]{0:T(256)S(1)}, bf16[128,8,128]{2,1,0:T(8,128)(2,1)S(1)}, s32[1024]{0:T(1024)S(1)}, bf16[128,1024]{1,0:T(8,128)(2,1)S(1)}, ...), branch_computations={%region_5.6_spmd, %region_6.7_spmd, %region_7.8_spmd, %region_8.9_... | conditional | bytes 6291520 | solution.py:541
  23.7 0.9 gather.6
  24.5 21.9 %all_to_all.45 = bf16[128,24,128]{2,1,0:T(8,128)(2,1)S(1)} all-to-all(bf16[128,24,128]{2,1,0:T(8,128)(2,1)S(1)} %gather.6), channel_id=1, replica_groups=mesh['dp'=128] {'dp'}, dimensions={0} | all-to-all | bytes 1572864 | tf_op jit(solution)/shard_map/cond/branch_2_fun/all_to_all | solution.py:362
  46.4 1.6 %rows.5 = (bf16[128,56,128]{2,1,0:T(8,128)(2,1)S(1)}, f32[2,128,128]{2,1,0:T(8,128)S(1)}, f32[128,1]{1,0:T(8,128)S(1)}, bf16[384,1024]{1,0:T(8,128)(2,1)S(1)}) custom-call(s32[1024]{0:T(1024)S(1)} %get-tuple-element.140.table_any, bf16[128,1024]{1,0:T(8,128)(2,1)S(1)} %get-tuple-element.137.qu_ref, bf16[128,1024]{1,0:T(8,128)(2,1)S(1)} %get-tuple-element.138.du_ref, ...), custom_call_target="tpu_custom_call" | custom-call | tf_op jit(solution)/shard_map/cond/branch_2_fun/rows/pallas_call | solution.py:39
  48.0 32.0 %all_to_all.46.recv_ref = bf16[128,56,128]{2,1,0:T(8,128)(2,1)S(1)} all-to-all(bf16[128,56,128]{2,1,0:T(8,128)(2,1)S(1)} %get-tuple-element.144), channel_id=1, replica_groups=mesh['dp'=128] {'dp'}, dimensions={0} | all-to-all | bytes 3670016 | tf_op jit(solution)/shard_map/cond/branch_2_fun/all_to_all | solution.py:362
  80.0 1.7 %docs.5 = (f32[128,1024]{1,0:T(8,128)S(1)}, bf16[128,1024]{1,0:T(8,128)(2,1)S(1)}, f32[16,128]{1,0:T(8,128)S(1)}) custom-call(s32[128]{0:T(128)S(1)} %get-tuple-element.134.info_any, bf16[128,1024]{1,0:T(8,128)(2,1)S(1)} %get-tuple-element.135.other_any, bf16[16,1024]{1,0:T(8,128)(2,1)S(1)} %get-tuple-element.136.pick_ref, ...), custom_call_target="tpu_custom_call" | custom-call | tf_op jit(solution)/shard_map/cond/branch_2_fun/docs/pallas_call | solution.py:39
  81.8 1.3 %collective-permute-start.2 = (bf16[128,1024]{1,0:T(8,128)(2,1)S(1)}, bf16[128,1024]{1,0:T(8,128)(2,1)S(1)}, u32[]{:S(2)}, u32[]{:S(2)}) collective-permute-start(bf16[128,1024]{1,0:T(8,128)(2,1)S(1)} %get-tuple-element.153), channel_id=1, source_target_pairs={{0,1},{1,0},{2,3},{3,2},{4,5},{5,4},{6,7},{7,6},{8,9},{9,8},{10,11... | collective-permute-start | bytes 786440 | tf_op jit(solution)/shard_map/cond/branch_2_fun/ppermute | solution.py:514
  83.1 1.3 %queries.5 = f32[128,1024]{1,0:T(8,128)} custom-call(f32[16,128]{1,0:T(8,128)S(1)} %get-tuple-element.145.sums_ref, bf16[128,1024]{1,0:T(8,128)(2,1)S(1)} %get-tuple-element.146.q_ref, f32[128,2]{1,0:T(8,128)S(1)} %get-tuple-element.147.inv_ref, f32[128,128]{1,0:T(8,128)S(1)} %get-tuple-element.141.e_own_ref, f32[2,128,128]{2,1,0:T(8,128)S(1)} %get-tuple-element.148.e_ref, ...), custom_call_target="tpu_custom_call" | custom-call | tf_op jit(solution)/shard_map/cond/branch_2_fun/queries/pallas_call | solution.py:39
  84.4 1.0 %final.6 = f32[128,1024]{1,0:T(8,128)} custom-call(bf16[128,1024]{1,0:T(8,128)(2,1)S(1)} %get-tuple-element.151.d_ref, f32[128,2]{1,0:T(8,128)S(1)} %get-tuple-element.147.inv_ref, f32[128,1024]{1,0:T(8,128)S(1)} %get-tuple-element.152.acc_ref, bf16[128,1024]{1,0:T(8,128)(2,1)S(1)} %collective-permute-done.2.swapped_ref), custom_call_target="tpu_custom_call" | custom-call | tf_op jit(solution)/shard_map/cond/branch_2_fun/final/pallas_call | solution.py:39
  (35 shorter events, 1.5 us)
Async XLA Ops:
  0.6 23.0 %copy-start = (bf16[128,1024]{1,0:T(8,128)(2,1)S(1)}, bf16[128,1024]{1,0:T(8,128)(2,1)}, u32[]{:S(2)}) copy-start(bf16[128,1024]{1,0:T(8,128)(2,1)} %d_ref.1) | copy-start | bytes 786436
  0.6 23.0 %copy-start.1 = (bf16[128,1024]{1,0:T(8,128)(2,1)S(1)}, bf16[128,1024]{1,0:T(8,128)(2,1)}, u32[]{:S(2)}) copy-start(bf16[128,1024]{1,0:T(8,128)(2,1)} %q_ref.1) | copy-start | bytes 786436
  0.6 22.3 %all-to-all-start.9 = ((bf16[128,8,128]{2,1,0:T(8,128)(2,1)}), bf16[128,8,128]{2,1,0:T(8,128)(2,1)S(1)}, u32[]{:S(2)}, u32[]{:S(2)}) async-start(bf16[128,8,128]{2,1,0:T(8,128)(2,1)} %bitcast.44), calls=%async_computation.9 | async-start | bytes 524288 | tf_op jit(solution)/shard_map/all_to_all | solution.py:362
  13.6 9.3 %collective-permute-start.3 = (bf16[128,1024]{1,0:T(8,128)(2,1)S(1)}, bf16[128,1024]{1,0:T(8,128)(2,1)S(1)}, u32[]{:S(2)}, u32[]{:S(2)}) collective-permute-start(bf16[128,1024]{1,0:T(8,128)(2,1)S(1)} %get-tuple-element.195), channel_id=1, source_target_pairs={{0,1},{1,0},{2,3},{3,2},{4,5},{5,4},{6,7},{7,6},{8,9},{9,8},{10,11... | collective-permute-start | bytes 786440 | tf_op jit(solution)/shard_map/ppermute | solution.py:514
  81.8 2.6 %collective-permute-start.2 = (bf16[128,1024]{1,0:T(8,128)(2,1)S(1)}, bf16[128,1024]{1,0:T(8,128)(2,1)S(1)}, u32[]{:S(2)}, u32[]{:S(2)}) collective-permute-start(bf16[128,1024]{1,0:T(8,128)(2,1)S(1)} %get-tuple-element.153), channel_id=1, source_target_pairs={{0,1},{1,0},{2,3},{3,2},{4,5},{5,4},{6,7},{7,6},{8,9},{9,8},{10,11... | collective-permute-start | bytes 786440 | tf_op jit(solution)/shard_map/cond/branch_2_fun/ppermute | solution.py:514

commit v8 on v6

--- a/solution.py
+++ b/solution.py
@@ -499,7 +499,7 @@
         n_any=2,
     )(info, other, picks, qu, du, et_own, recv)
     swapped = swap_cores(partner)
-    grad_scratch = (pltpu.VMEM((rows, features), f32), pltpu.SemaphoreType.DMA((4,)))
+    grad_scratch = (pltpu.VMEM((rows, features), f32), pltpu.SemaphoreType.DMA((2,)))
     grad_query = vmem_call(
         query_side_kernel, grad, 0, 7, grad_scratch, name="queries", out_space=pl.ANY
     )(sums, query_emb, inv, e_own, e, row_total, doc_units)

time: 83.2 us -> 81.6 us (0.981); the launches traced: 82.9 us -> 82.9 us
  no operation moved by 1% of the time
where the time goes in v8:
time: 81.6 us; the launch traced here: 82.9 us
  blocking collectives  51.1 us (63%)
  starting transfers between devices  13.9 us (17%)
  Pallas kernels  7.83 us (10%)
  waiting for transfers between devices  3.15 us (4%)
  local copies, waits for them, and re-layouts  2.54 us (3%)
  other arithmetic  2.37 us (3%)
  between operations  1.65 us (2%)
    all_to_all x2, blocking collectives, exchange(): return lax.all_to_all(x, 'dp', split_axis=0, concat_axis=0, tiled=True)  51.1 us
    all_to_all x1, starting transfers between devices, exchange(): return lax.all_to_all(x, 'dp', split_axis=0, concat_axis=0, tiled=True)  11.5 us
    pallas_call x5, Pallas kernels, run(): return call(*args[:n_smem + n_any], *kept)  6.34 us
    all_to_all x1, waiting for transfers between devices, exchange(): return lax.all_to_all(x, 'dp', split_axis=0, concat_axis=0, tiled=True)  3.14 us
    ppermute x2, starting transfers between devices, swap_cores(): lax.ppermute(x, 'dp', [(i, i ^ 1) for i in range(lax.axis_size('dp'))])  2.46 us
  transfers between devices with their start and end apart: 3, of which 1 were waited for; matrix products, arithmetic and copies ran while one was open for 6% of the time, Pallas kernels for 3%

profile of v8, /device:TPU:1, one launch (start us, length us, event | category | flops | bytes accessed | tf_op | source)
XLA Modules:
  0.0 82.9 jit_solution(11561635046905598008)
XLA Ops:
  0.6 11.5 %all-to-all-start.9 = ((bf16[128,8,128]{2,1,0:T(8,128)(2,1)}), bf16[128,8,128]{2,1,0:T(8,128)(2,1)S(1)}, u32[]{:S(2)}, u32[]{:S(2)}) async-start(bf16[128,8,128]{2,1,0:T(8,128)(2,1)} %bitcast.44), calls=%async_computation.9 | async-start | bytes 524288 | tf_op jit(solution)/shard_map/all_to_all | solution.py:361
  12.1 1.5 %own.1 = (bf16[128,1024]{1,0:T(8,128)(2,1)S(1)}, bf16[128,1024]{1,0:T(8,128)(2,1)S(1)}, f32[128,2]{1,0:T(8,128)S(1)}, f32[128,128]{1,0:T(8,128)S(1)}, f32[128,128]{1,0:T(8,128)S(1)}) custom-call(bf16[128,1024]{1,0:T(8,128)(2,1)} %q_ref.1, bf16[128,1024]{1,0:T(8,128)(2,1)} %d_ref.1), custom_call_target="tpu_custom_call" | custom-call | tf_op jit(solution)/shard_map/own/pallas_call | solution.py:37
  13.6 1.1 %collective-permute-start.3 = (bf16[128,1024]{1,0:T(8,128)(2,1)S(1)}, bf16[128,1024]{1,0:T(8,128)(2,1)S(1)}, u32[]{:S(2)}, u32[]{:S(2)}) collective-permute-start(bf16[128,1024]{1,0:T(8,128)(2,1)S(1)} %get-tuple-element.195), channel_id=1, source_target_pairs={{0,1},{1,0},{2,3},{3,2},{4,5},{5,4},{6,7},{7,6},{8,9},{9,8},{10,11... | collective-permute-start | bytes 786440 | tf_op jit(solution)/shard_map/ppermute | solution.py:513
  14.8 0.8 fusion.20
  15.6 0.7 iota_compare_fusion.3
  16.3 0.1 lt.75
  16.9 0.1 select_reduce_fusion.2
  17.2 0.2 dynamic-slice_reduce_fusion
  17.4 0.1 reshape.287
  17.5 0.2 convert_reduce_fusion
  17.7 0.6 fusion.16
  18.4 0.2 select_reduce_fusion
  18.6 0.1 reshape.288
  18.9 0.1 reshape.290
  19.8 3.1 %all-to-all-done.9 = bf16[128,8,128]{2,1,0:T(8,128)(2,1)S(1)} async-done(((bf16[128,8,128]{2,1,0:T(8,128)(2,1)}), bf16[128,8,128]{2,1,0:T(8,128)(2,1)S(1)}, u32[]{:S(2)}, u32[]{:S(2)}) %all-to-all-start.9) | async-done | bytes 262176 | tf_op jit(solution)/shard_map/all_to_all | solution.py:361
  23.6 59.1 %conditional.1 = ((f32[128,1024]{1,0:T(8,128)}, f32[128,1024]{1,0:T(8,128)})) conditional(s32[]{:T(128)} %clamp.3, (bf16[128,1024]{1,0:T(8,128)(2,1)S(1)}, s32[256]{0:T(256)S(1)}, bf16[128,8,128]{2,1,0:T(8,128)(2,1)S(1)}, s32[1024]{0:T(1024)S(1)}, bf16[128,1024]{1,0:T(8,128)(2,1)S(1)}, ...), branch_computations={%region_5.6_spmd, %region_6.7_spmd, %region_7.8_spmd, %region_8.9_... | conditional | bytes 6291520 | solution.py:540
  23.7 0.9 %gather.5 = bf16[128,24,128]{2,1,0:T(8,128)(2,1)S(1)} custom-call(s32[256]{0:T(256)S(1)} %get-tuple-element.122.cols_any, bf16[128,8,128]{2,1,0:T(8,128)(2,1)S(1)} %get-tuple-element.123.spread_ref, bf16[128,8,128]{2,1,0:T(8,128)(2,1)S(1)} %bitcast.41), custom_call_target="tpu_custom_call" | custom-call | tf_op jit(solution)/shard_map/cond/branch_1_fun/gather/pallas_call | solution.py:39
  24.5 21.9 %all_to_all.43 = bf16[128,24,128]{2,1,0:T(8,128)(2,1)S(1)} all-to-all(bf16[128,24,128]{2,1,0:T(8,128)(2,1)S(1)} %gather.5), channel_id=1, replica_groups=mesh['dp'=128] {'dp'}, dimensions={0} | all-to-all | bytes 1572864 | tf_op jit(solution)/shard_map/cond/branch_1_fun/all_to_all | solution.py:361
  46.4 1.5 %rows.4 = (bf16[128,48,128]{2,1,0:T(8,128)(2,1)S(1)}, f32[2,128,128]{2,1,0:T(8,128)S(1)}, f32[128,1]{1,0:T(8,128)S(1)}, bf16[384,1024]{1,0:T(8,128)(2,1)S(1)}) custom-call(s32[1024]{0:T(1024)S(1)} %get-tuple-element.120.table_any, bf16[128,1024]{1,0:T(8,128)(2,1)S(1)} %get-tuple-element.117.qu_ref, bf16[128,1024]{1,0:T(8,128)(2,1)S(1)} %get-tuple-element.118.du_ref, ...), custom_call_target="tpu_custom_call" | custom-call | tf_op jit(solution)/shard_map/cond/branch_1_fun/rows/pallas_call | solution.py:39
  47.9 29.2 %all_to_all.44.recv_ref = bf16[128,48,128]{2,1,0:T(8,128)(2,1)S(1)} all-to-all(bf16[128,48,128]{2,1,0:T(8,128)(2,1)S(1)} %get-tuple-element.124), channel_id=1, replica_groups=mesh['dp'=128] {'dp'}, dimensions={0} | all-to-all | bytes 3145728 | tf_op jit(solution)/shard_map/cond/branch_1_fun/all_to_all | solution.py:361
  77.1 1.7 %docs.4 = (f32[128,1024]{1,0:T(8,128)S(1)}, bf16[128,1024]{1,0:T(8,128)(2,1)S(1)}, f32[16,128]{1,0:T(8,128)S(1)}) custom-call(s32[128]{0:T(128)S(1)} %get-tuple-element.114.info_any, bf16[128,1024]{1,0:T(8,128)(2,1)S(1)} %get-tuple-element.115.other_any, bf16[16,1024]{1,0:T(8,128)(2,1)S(1)} %get-tuple-element.116.pick_ref, ...), custom_call_target="tpu_custom_call" | custom-call | tf_op jit(solution)/shard_map/cond/branch_1_fun/docs/pallas_call | solution.py:39
  78.8 1.3 %collective-permute-start.1 = (bf16[128,1024]{1,0:T(8,128)(2,1)S(1)}, bf16[128,1024]{1,0:T(8,128)(2,1)S(1)}, u32[]{:S(2)}, u32[]{:S(2)}) collective-permute-start(bf16[128,1024]{1,0:T(8,128)(2,1)S(1)} %get-tuple-element.133), channel_id=1, source_target_pairs={{0,1},{1,0},{2,3},{3,2},{4,5},{5,4},{6,7},{7,6},{8,9},{9,8},{10,11... | collective-permute-start | bytes 786440 | tf_op jit(solution)/shard_map/cond/branch_1_fun/ppermute | solution.py:513
  80.1 1.3 %queries.4 = f32[128,1024]{1,0:T(8,128)} custom-call(f32[16,128]{1,0:T(8,128)S(1)} %get-tuple-element.125.sums_ref, bf16[128,1024]{1,0:T(8,128)(2,1)S(1)} %get-tuple-element.126.q_ref, f32[128,2]{1,0:T(8,128)S(1)} %get-tuple-element.127.inv_ref, f32[128,128]{1,0:T(8,128)S(1)} %get-tuple-element.121.e_own_ref, f32[2,128,128]{2,1,0:T(8,128)S(1)} %get-tuple-element.128.e_ref, ...), custom_call_target="tpu_custom_call" | custom-call | tf_op jit(solution)/shard_map/cond/branch_1_fun/queries/pallas_call | solution.py:39
  81.4 1.0 %final.5 = f32[128,1024]{1,0:T(8,128)} custom-call(bf16[128,1024]{1,0:T(8,128)(2,1)S(1)} %get-tuple-element.131.d_ref, f32[128,2]{1,0:T(8,128)S(1)} %get-tuple-element.127.inv_ref, f32[128,1024]{1,0:T(8,128)S(1)} %get-tuple-element.132.acc_ref, bf16[128,1024]{1,0:T(8,128)(2,1)S(1)} %collective-permute-done.1.swapped_ref), custom_call_target="tpu_custom_call" | custom-call | tf_op jit(solution)/shard_map/cond/branch_1_fun/final/pallas_call | solution.py:39
  (35 shorter events, 1.5 us)
Async XLA Ops:
  0.6 23.0 %copy-start = (bf16[128,1024]{1,0:T(8,128)(2,1)S(1)}, bf16[128,1024]{1,0:T(8,128)(2,1)}, u32[]{:S(2)}) copy-start(bf16[128,1024]{1,0:T(8,128)(2,1)} %d_ref.1) | copy-start | bytes 786436
  0.6 23.0 %copy-start.1 = (bf16[128,1024]{1,0:T(8,128)(2,1)S(1)}, bf16[128,1024]{1,0:T(8,128)(2,1)}, u32[]{:S(2)}) copy-start(bf16[128,1024]{1,0:T(8,128)(2,1)} %q_ref.1) | copy-start | bytes 786436
  0.6 22.3 %all-to-all-start.9 = ((bf16[128,8,128]{2,1,0:T(8,128)(2,1)}), bf16[128,8,128]{2,1,0:T(8,128)(2,1)S(1)}, u32[]{:S(2)}, u32[]{:S(2)}) async-start(bf16[128,8,128]{2,1,0:T(8,128)(2,1)} %bitcast.44), calls=%async_computation.9 | async-start | bytes 524288 | tf_op jit(solution)/shard_map/all_to_all | solution.py:361
  13.6 9.3 %collective-permute-start.3 = (bf16[128,1024]{1,0:T(8,128)(2,1)S(1)}, bf16[128,1024]{1,0:T(8,128)(2,1)S(1)}, u32[]{:S(2)}, u32[]{:S(2)}) collective-permute-start(bf16[128,1024]{1,0:T(8,128)(2,1)S(1)} %get-tuple-element.195), channel_id=1, source_target_pairs={{0,1},{1,0},{2,3},{3,2},{4,5},{5,4},{6,7},{7,6},{8,9},{9,8},{10,11... | collective-permute-start | bytes 786440 | tf_op jit(solution)/shard_map/ppermute | solution.py:513
  78.8 2.7 %collective-permute-start.1 = (bf16[128,1024]{1,0:T(8,128)(2,1)S(1)}, bf16[128,1024]{1,0:T(8,128)(2,1)S(1)}, u32[]{:S(2)}, u32[]{:S(2)}) collective-permute-start(bf16[128,1024]{1,0:T(8,128)(2,1)S(1)} %get-tuple-element.133), channel_id=1, source_target_pairs={{0,1},{1,0},{2,3},{3,2},{4,5},{5,4},{6,7},{7,6},{8,9},{9,8},{10,11... | collective-permute-start | bytes 786440 | tf_op jit(solution)/shard_map/cond/branch_1_fun/ppermute | solution.py:513
